TPU v7x, 256 devices: a whole 4x4x8 slice. The times are simulated.
256 devices in a mesh: lon: 16 (over z, y_lo), lat: 8 (over x, y_hi), lev: 2 (over core).
Axes of the slice: x: 4, y: 4 (y_hi: 2, y_lo: 2; y = y_hi * 2 + y_lo), z: 8, core: 2. Of those that a mesh axis runs over, the one named last changes fastest.
Arguments:
- adjoint_in: float32 [9, 16, 128, 2048], P(None, 'lev', 'lat', 'lon'), may hold values from -6 to 6
- trajectory: bfloat16 [3, 9, 16, 128, 2048], P(None, None, 'lev', 'lat', 'lon'), may hold values from 0.5 to 2
- courant: float32 [2, 16, 128, 2048], P(None, 'lev', 'lat', 'lon'), may hold values from -0.4 to 0.4
- mixing: float32 [16, 128, 2048], P('lev', 'lat', 'lon'), may hold values from 0.02 to 0.2
- coag_rates: float32 [6, 16], replicated, may hold values from 0.02 to 0.2
- settle_speed: float32 [8, 9], replicated, may hold values from 0.01 to 0.2
- settle_class: int32 [16], replicated, may hold values from 0 to 7
- emis_profile: float32 [16], replicated, may hold values from 0.1 to 1
- emis_coef: float32 [9], replicated, may hold values from 0.5 to 2
- land_mask: int32 [128, 2048], P('lat', 'lon'), may hold values 0 or 1
- source_mask: int32 [128, 2048], P('lat', 'lon'), may hold values 0 or 1
Outputs:
- adjoint_out: float32 [9, 16, 128, 2048], P(None, 'lev', 'lat', 'lon')
- emis_grad: float32 [3, 128, 2048], P(None, 'lat', 'lon')
All inputs are finite; a program needn't handle non-finite values. No bound on the sum of `land_mask` or of `source_mask` on one device may be relied on, other than what follows from the above.
Results may differ from a plain program's by a relative error of at most 0.0003.
Values may be sent and summed in bfloat16 or wider, within the bound.
A program may use at most 64 MiB of HBM per device.

v0:
```python
import jax
import jax.numpy as jnp
from jax import lax
from jax.sharding import PartitionSpec as P


def with_halo(cells, sides, width, closed):
    for axis, dim in sides:
        count = lax.axis_size(axis)
        ends = count if closed else count - 1
        head = lax.slice_in_dim(cells, 0, width, axis=dim)
        tail = lax.slice_in_dim(cells, cells.shape[dim] - width, cells.shape[dim], axis=dim)
        cells = jnp.concatenate(
            [
                lax.ppermute(tail, axis, [(i, (i + 1) % count) for i in range(ends)]),
                cells,
                lax.ppermute(head, axis, [((i + 1) % count, i) for i in range(ends)]),
            ],
            axis=dim,
        )
    return cells


def slab(field, axis, start, length):
    return lax.slice_in_dim(field, start, start + length, axis=axis)


def transport(padded, courant_pad, axis, length):
    courant_wide = courant_pad[None]
    diff_face = slab(padded, axis, 0, length + 3) - slab(padded, axis, 1, length + 3)
    face_speed = slab(courant_wide, axis, 0, length + 3)
    forward_part = jnp.maximum(face_speed, 0.0) * diff_face
    backward_part = jnp.minimum(face_speed, 0.0) * diff_face
    return (
        -1.5 * slab(forward_part, axis, 2, length)
        + 0.5 * slab(forward_part, axis, 3, length)
        - 1.5 * slab(backward_part, axis, 1, length)
        + 0.5 * slab(backward_part, axis, 0, length)
    )


def vertical(padded, mixing_pad, speeds, deposit):
    depth_count = padded.shape[1] - 2
    mixing_below = mixing_pad[:depth_count]
    mixing_above = mixing_pad[1 : depth_count + 1]
    speed_level = speeds[:, :, None, None]
    centre = padded[:, 1 : depth_count + 1]
    return (
        centre * (1.0 - mixing_above - mixing_below - speed_level - deposit)
        + padded[:, :depth_count] * (mixing_below + speed_level)
        + padded[:, 2:] * mixing_above
    )


def coag_increment(state, rates):
    rate_grid = rates[:, :, None, None]
    number = [state[0], state[3], state[6]]
    volume = [state[1], state[4], state[7]]
    moment_six = [state[2], state[5], state[8]]
    pair_rate = {(0, 1): rate_grid[3], (0, 2): rate_grid[4], (1, 2): rate_grid[5]}
    outputs = []
    for mode_index in range(3):
        d_number = -rate_grid[mode_index] * number[mode_index] * number[mode_index]
        d_volume = jnp.zeros_like(number[mode_index])
        d_moment = rate_grid[mode_index] * volume[mode_index] * volume[mode_index]
        for other_mode in range(3):
            if other_mode > mode_index:
                pair = pair_rate[mode_index, other_mode]
                d_number = d_number - pair * number[mode_index] * number[other_mode]
                d_volume = d_volume - pair * volume[mode_index] * number[other_mode]
                d_moment = d_moment - pair * moment_six[mode_index] * number[other_mode]
            if other_mode < mode_index:
                pair = pair_rate[other_mode, mode_index]
                d_volume = d_volume + pair * volume[other_mode] * number[mode_index]
                d_moment = d_moment + pair * (
                    moment_six[other_mode] * number[mode_index]
                    + 2.0 * volume[other_mode] * volume[mode_index]
                )
        outputs.extend([d_number, d_volume, d_moment])
    return jnp.stack(outputs)


def coag_adjoint(adjoint, state, rates):
    primal_out, pullback = jax.vjp(lambda value: coag_increment(value, rates), state)
    return adjoint + pullback(adjoint)[0]


def emission_part(adjoint, profile, emis_coef, source):
    weighted = adjoint * (emis_coef[:, None, None, None] * profile[None, :, None, None])
    per_tracer = jnp.sum(weighted, axis=1)
    per_mode = jnp.sum(per_tracer.reshape(3, 3, per_tracer.shape[1], per_tracer.shape[2]), axis=1)
    return per_mode * source


def sides(field, lat_index, row_count, lat_count):
    lon_pad = with_halo(field, (("lon", 3),), 2, True)
    lat_pad = with_halo(field, (("lat", 2),), 2, False)
    return (lon_pad, lat_pad)


def planes(field):
    return with_halo(field, (("lev", 1),), 1, False)


def run_split(
    adjoint_in,
    trajectory,
    winds,
    mixing_top,
    coag_rates,
    speeds_all,
    emis_profile,
    emis_coef,
    dep_rows,
    source,
):
    depth_count = adjoint_in.shape[1]
    row_count = adjoint_in.shape[2]
    col_count = adjoint_in.shape[3]
    lev_index = lax.axis_index("lev")
    lat_index = lax.axis_index("lat")
    lat_count = lax.axis_size("lat")
    level_global = lev_index * depth_count + jnp.arange(depth_count, dtype=jnp.int32)
    level_start = lev_index * depth_count
    rates_own = lax.dynamic_slice_in_dim(coag_rates, level_start, depth_count, 1)
    profile_own = lax.dynamic_slice_in_dim(emis_profile, level_start, depth_count, 0)
    wind_lon, wind_lat = sides(winds, lat_index, row_count, lat_count)
    east_pad = wind_lon[0]
    north_pad = wind_lat[1]
    mixing_pad = planes(mixing_top[None])[0]
    speeds_used = lax.dynamic_slice_in_dim(speeds_all, level_start, depth_count, 1)
    surface = (level_global == 0).astype(jnp.float32)
    deposit = dep_rows[None] * surface[:, None, None]
    adjoint = adjoint_in
    emis_grad = jnp.zeros((3, row_count, col_count), jnp.float32)
    for step_index in range(trajectory.shape[0] - 1, -1, -1):
        emis_grad = emis_grad + emission_part(adjoint, profile_own, emis_coef, source)
        adjoint = coag_adjoint(adjoint, trajectory[step_index].astype(jnp.float32), rates_own)
        adjoint = vertical(planes(adjoint), mixing_pad, speeds_used, deposit)
        lon_pad, lat_pad = sides(adjoint, lat_index, row_count, lat_count)
        adjoint = (
            adjoint
            + transport(lon_pad, east_pad, 3, col_count)
            + transport(lat_pad, north_pad, 2, row_count)
        )
    emis_grad = lax.psum(emis_grad, "lev")
    return (adjoint, emis_grad)


def shards(
    adjoint_in,
    trajectory,
    courant,
    mixing,
    coag_rates,
    settle_speed,
    settle_class,
    emis_profile,
    emis_coef,
    land_mask,
    source_mask,
):
    depth_count = adjoint_in.shape[1]
    row_count = adjoint_in.shape[2]
    lev_index = lax.axis_index("lev")
    lat_index = lax.axis_index("lat")
    lat_count = lax.axis_size("lat")
    level_total = settle_class.shape[0]
    row_global = lat_index * row_count + jnp.arange(row_count, dtype=jnp.int32)
    top_row = (row_global == row_count * lat_count - 1)[None, :, None]
    winds = jnp.stack([courant[0], jnp.where(top_row, 0.0, courant[1])])
    level_global = lev_index * depth_count + jnp.arange(depth_count, dtype=jnp.int32)
    mixing_top = jnp.where((level_global == level_total - 1)[:, None, None], 0.0, mixing)
    choose = (
        settle_class[:, None] == jnp.arange(settle_speed.shape[0], dtype=jnp.int32)[None, :]
    ).astype(jnp.float32)
    speeds_all = jnp.dot(choose, settle_speed, precision=lax.Precision.HIGHEST).T
    dep_rows = 0.1 + 0.3 * land_mask.astype(jnp.float32)
    source = source_mask.astype(jnp.float32)
    return run_split(
        adjoint_in,
        trajectory,
        winds,
        mixing_top,
        coag_rates,
        speeds_all,
        emis_profile,
        emis_coef,
        dep_rows,
        source,
    )


def solution(mesh):
    return jax.shard_map(
        shards,
        mesh=mesh,
        in_specs=(
            P(None, "lev", "lat", "lon"),
            P(None, None, "lev", "lat", "lon"),
            P(None, "lev", "lat", "lon"),
            P("lev", "lat", "lon"),
            P(),
            P(),
            P(),
            P(),
            P(),
            P("lat", "lon"),
            P("lat", "lon"),
        ),
        out_specs=(P(None, "lev", "lat", "lon"), P(None, "lat", "lon")),
        check_vma=False,
    )
```

profile of v0, /device:TPU:5, one launch (start us, length us, event | category | flops | bytes accessed | tf_op | source)
XLA Modules:
  0.0 129.6 jit_solution(11100671563132194854)
XLA Ops:
  0.7 0.8 constant_dynamic-slice_fusion
  1.5 1.4 %slice_convert_fusion = (f32[1,9,8,16,128]{4,3,2,1,0:T(8,128)S(1)}, f32[1,9,8,16,128]{4,3,2,1,0:T(8,128)S(1)}, f32[1,9,8,16,128]{4,3,2,1,0:T(8,128)S(1)}) fusion(bf16[3,9,8,16,128]{4,3,2,1,0:T(8,128)(2,1)} %param.12), kind=kLoop, calls=%fused_computation.97 | loop fusion | flops 442368 | bytes 2654208 | tf_op jit(solution)/shard_map/convert_element_type | solution.py:138
  3.8 0.7 fusion.59
  4.4 1.3 collective-permute-start.1
  5.7 3.0 %collective-permute-start.2 = (f32[9,1,16,128]{3,2,1,0:T(8,128)}, f32[9,1,16,128]{3,2,1,0:T(8,128)S(1)}, u32[]{:S(2)}, u32[]{:S(2)}) collective-permute-start(f32[9,1,16,128]{3,2,1,0:T(8,128)} %get-tuple-element.55), channel_id=1, source_target_pairs={{1,0},{3,2},{5,4},{7,6},{9,8},{11,10},{13,12},{15,14},{17,16},{19,... | collective-permute-start | bytes 221192 | tf_op jit(solution)/shard_map/ppermute | solution.py:17
  8.9 1.3 collective-permute-start
  10.4 1.4 %collective-permute-start.3 = (f32[2,8,16,2]{3,2,1,0:T(8,128)S(1)}, f32[2,8,16,2]{3,2,1,0:T(8,128)S(1)}, u32[]{:S(2)}, u32[]{:S(2)}) collective-permute-start(f32[2,8,16,2]{3,2,1,0:T(8,128)S(1)} %get-tuple-element.60), channel_id=1, source_target_pairs={{0,16},{16,32},{32,48},{48,64},{64,80},{80,96},{96,112},{112,128},... | collective-permute-start | bytes 6152 | tf_op jit(solution)/shard_map/ppermute | solution.py:15
  11.7 5.4 %collective-permute-start.4 = (f32[2,8,16,2]{3,2,1,0:T(8,128)S(1)}, f32[2,8,16,2]{3,2,1,0:T(8,128)S(1)}, u32[]{:S(2)}, u32[]{:S(2)}) collective-permute-start(f32[2,8,16,2]{3,2,1,0:T(8,128)S(1)} %get-tuple-element.61), channel_id=1, source_target_pairs={{16,0},{32,16},{48,32},{64,48},{80,64},{96,80},{112,96},{128,112},... | collective-permute-start | bytes 6152 | tf_op jit(solution)/shard_map/ppermute | solution.py:17
  17.6 0.7 dynamic_slice.11
  18.3 1.4 %collective-permute-done.3 = f32[2,8,16,2]{3,2,1,0:T(8,128)S(1)} collective-permute-done((f32[2,8,16,2]{3,2,1,0:T(8,128)S(1)}, f32[2,8,16,2]{3,2,1,0:T(8,128)S(1)}, u32[]{:S(2)}, u32[]{:S(2)}) %collective-permute-start.3) | collective-permute-done | bytes 2080 | tf_op jit(solution)/shard_map/ppermute | solution.py:15
  19.7 4.5 %collective-permute-start.7 = (f32[2,8,2,128]{3,2,1,0:T(2,128)S(1)}, f32[2,8,2,128]{3,2,1,0:T(2,128)S(1)}, u32[]{:S(2)}, u32[]{:S(2)}) collective-permute-start(f32[2,8,2,128]{3,2,1,0:T(2,128)S(1)} %get-tuple-element.62), channel_id=1, source_target_pairs={{0,2},{2,4},{4,6},{6,8},{8,10},{10,12},{12,14},{1,3},{3,5},{5,7},{... | collective-permute-start | bytes 49160 | tf_op jit(solution)/shard_map/ppermute | solution.py:15
  24.3 3.2 %collective-permute-start.8 = (f32[2,8,2,128]{3,2,1,0:T(2,128)S(1)}, f32[2,8,2,128]{3,2,1,0:T(2,128)S(1)}, u32[]{:S(2)}, u32[]{:S(2)}) collective-permute-start(f32[2,8,2,128]{3,2,1,0:T(2,128)S(1)} %get-tuple-element.63), channel_id=1, source_target_pairs={{2,0},{4,2},{6,4},{8,6},{10,8},{12,10},{14,12},{3,1},{5,3},{7,5},{... | collective-permute-start | bytes 49160 | tf_op jit(solution)/shard_map/ppermute | solution.py:17
  27.6 0.7 fusion.35
  28.3 1.9 %collective-permute-done.8 = f32[2,8,2,128]{3,2,1,0:T(2,128)S(1)} collective-permute-done((f32[2,8,2,128]{3,2,1,0:T(2,128)S(1)}, f32[2,8,2,128]{3,2,1,0:T(2,128)S(1)}, u32[]{:S(2)}, u32[]{:S(2)}) %collective-permute-start.8) | collective-permute-done | bytes 16416 | tf_op jit(solution)/shard_map/ppermute | solution.py:17
  30.3 0.7 maximum_bitcast_fusion.1
  31.0 0.6 copy-done.16
  31.6 1.1 fusion.1
  32.8 1.2 fusion.57
  34.0 2.2 %copy.101 = f32[9,8,16,2]{2,1,3,0:T(8,128)} copy(f32[9,8,16,2]{3,2,1,0:T(8,128)} %get-tuple-element.50) | data formatting | bytes 18432 | tf_op jit(solution)/shard_map/slice | solution.py:12
  36.2 2.2 %copy.102 = f32[9,8,16,2]{2,1,3,0:T(8,128)} copy(f32[9,8,16,2]{3,2,1,0:T(8,128)} %get-tuple-element.51) | data formatting | bytes 18432 | tf_op jit(solution)/shard_map/slice | solution.py:11
  38.3 3.6 %collective-permute-start.6 = (f32[9,8,16,2]{2,1,3,0:T(8,128)}, f32[9,8,16,2]{2,1,3,0:T(8,128)}, u32[]{:S(2)}, u32[]{:S(2)}) collective-permute-start(f32[9,8,16,2]{2,1,3,0:T(8,128)} %copy.102), channel_id=1, source_target_pairs={{16,0},{32,16},{48,32},{64,48},{80,64},{96,80},{112,96},{128,112},... | collective-permute-start | bytes 27656 | tf_op jit(solution)/shard_map/ppermute | solution.py:17
  42.0 0.6 copy.105
  42.6 3.8 %collective-permute-start.9 = (f32[9,8,2,128]{3,1,2,0:T(8,128)}, f32[9,8,2,128]{3,1,2,0:T(8,128)}, u32[]{:S(2)}, u32[]{:S(2)}) collective-permute-start(f32[9,8,2,128]{3,1,2,0:T(8,128)} %copy.105), channel_id=1, source_target_pairs={{0,2},{2,4},{4,6},{6,8},{8,10},{10,12},{12,14},{1,3},{3,5},{5,7},{... | collective-permute-start | bytes 221192 | tf_op jit(solution)/shard_map/ppermute | solution.py:15
  46.4 0.6 copy.106
  47.0 3.9 %collective-permute-start.10 = (f32[9,8,2,128]{3,1,2,0:T(8,128)}, f32[9,8,2,128]{3,1,2,0:T(8,128)}, u32[]{:S(2)}, u32[]{:S(2)}) collective-permute-start(f32[9,8,2,128]{3,1,2,0:T(8,128)} %copy.106), channel_id=1, source_target_pairs={{2,0},{4,2},{6,4},{8,6},{10,8},{12,10},{14,12},{3,1},{5,3},{7,5},{... | collective-permute-start | bytes 221192 | tf_op jit(solution)/shard_map/ppermute | solution.py:17
  50.9 2.2 %copy.103 = f32[9,8,16,2]{3,2,1,0:T(8,128)} copy(f32[9,8,16,2]{2,1,3,0:T(8,128)} %collective-permute-done.5) | data formatting | bytes 18432 | tf_op jit(solution)/shard_map/ppermute | solution.py:15
  53.2 2.2 %copy.104 = f32[9,8,16,2]{3,2,1,0:T(8,128)} copy(f32[9,8,16,2]{2,1,3,0:T(8,128)} %collective-permute-done.6) | data formatting | bytes 18432 | tf_op jit(solution)/shard_map/ppermute | solution.py:17
  55.3 1.8 %pad_maximum_fusion = f32[9,8,16,132]{3,2,1,0:T(8,128)S(1)} fusion(f32[9,8,16,2]{3,2,1,0:T(8,128)} %copy.104, f32[9,8,16,128]{3,2,1,0:T(8,128)S(1)} %fusion.1, f32[9,8,16,2]{3,2,1,0:T(8,128)} %copy.103), kind=kLoop, calls=%fused_computation.3 | loop fusion | flops 304128 | bytes 1216512 | tf_op jit(solution)/shard_map/concatenate | solution.py:13
  57.6 1.0 copy.107
  58.6 0.9 copy.108
  59.9 0.7 copy-done.17
  60.6 0.7 fusion.25
  62.5 1.3 collective-permute-start.11
  63.8 6.4 %collective-permute-start.12 = (f32[9,1,16,128]{3,2,1,0:T(8,128)S(1)}, f32[9,1,16,128]{3,2,1,0:T(8,128)S(1)}, u32[]{:S(2)}, u32[]{:S(2)}) collective-permute-start(f32[9,1,16,128]{3,2,1,0:T(8,128)S(1)} %get-tuple-element.49), channel_id=1, source_target_pairs={{1,0},{3,2},{5,4},{7,6},{9,8},{11,10},{13,12},{15,14},{17,16},{19,... | collective-permute-start | bytes 221192 | tf_op jit(solution)/shard_map/ppermute | solution.py:17
  70.3 0.8 collective-permute-done.12
  71.3 1.2 fusion.54
  72.5 2.2 %copy.109 = f32[9,8,16,2]{2,1,3,0:T(8,128)} copy(f32[9,8,16,2]{3,2,1,0:T(8,128)} %get-tuple-element.44) | data formatting | bytes 18432 | tf_op jit(solution)/shard_map/slice | solution.py:12
  74.7 2.2 %copy.110 = f32[9,8,16,2]{2,1,3,0:T(8,128)} copy(f32[9,8,16,2]{3,2,1,0:T(8,128)} %get-tuple-element.45) | data formatting | bytes 18432 | tf_op jit(solution)/shard_map/slice | solution.py:11
  76.9 3.6 %collective-permute-start.14 = (f32[9,8,16,2]{2,1,3,0:T(8,128)}, f32[9,8,16,2]{2,1,3,0:T(8,128)}, u32[]{:S(2)}, u32[]{:S(2)}) collective-permute-start(f32[9,8,16,2]{2,1,3,0:T(8,128)} %copy.110), channel_id=1, source_target_pairs={{16,0},{32,16},{48,32},{64,48},{80,64},{96,80},{112,96},{128,112},... | collective-permute-start | bytes 27656 | tf_op jit(solution)/shard_map/ppermute | solution.py:17
  80.5 0.6 copy.113
  81.2 3.9 %collective-permute-start.15 = (f32[9,8,2,128]{3,1,2,0:T(8,128)}, f32[9,8,2,128]{3,1,2,0:T(8,128)}, u32[]{:S(2)}, u32[]{:S(2)}) collective-permute-start(f32[9,8,2,128]{3,1,2,0:T(8,128)} %copy.113), channel_id=1, source_target_pairs={{0,2},{2,4},{4,6},{6,8},{8,10},{10,12},{12,14},{1,3},{3,5},{5,7},{... | collective-permute-start | bytes 221192 | tf_op jit(solution)/shard_map/ppermute | solution.py:15
  85.1 0.6 copy.114
  85.7 3.9 %collective-permute-start.16 = (f32[9,8,2,128]{3,1,2,0:T(8,128)}, f32[9,8,2,128]{3,1,2,0:T(8,128)}, u32[]{:S(2)}, u32[]{:S(2)}) collective-permute-start(f32[9,8,2,128]{3,1,2,0:T(8,128)} %copy.114), channel_id=1, source_target_pairs={{2,0},{4,2},{6,4},{8,6},{10,8},{12,10},{14,12},{3,1},{5,3},{7,5},{... | collective-permute-start | bytes 221192 | tf_op jit(solution)/shard_map/ppermute | solution.py:17
  89.7 2.2 %copy.111 = f32[9,8,16,2]{3,2,1,0:T(8,128)} copy(f32[9,8,16,2]{2,1,3,0:T(8,128)} %collective-permute-done.13) | data formatting | bytes 18432 | tf_op jit(solution)/shard_map/ppermute | solution.py:15
  91.9 2.2 %copy.112 = f32[9,8,16,2]{3,2,1,0:T(8,128)} copy(f32[9,8,16,2]{2,1,3,0:T(8,128)} %collective-permute-done.14) | data formatting | bytes 18432 | tf_op jit(solution)/shard_map/ppermute | solution.py:17
  94.1 1.8 %pad_maximum_fusion.1 = f32[9,8,16,132]{3,2,1,0:T(8,128)S(1)} fusion(f32[9,8,16,2]{3,2,1,0:T(8,128)} %copy.112, f32[9,8,16,128]{3,2,1,0:T(8,128)S(1)} %fusion.3, f32[9,8,16,2]{3,2,1,0:T(8,128)} %copy.111), kind=kLoop, calls=%fused_computation.4 | loop fusion | flops 304128 | bytes 1216512 | tf_op jit(solution)/shard_map/concatenate | solution.py:13
  95.9 0.5 broadcast_multiply_fusion.4
  96.4 1.0 copy.115
  97.4 0.9 copy.116
  98.7 0.6 copy-done.10
  99.4 1.6 %multiply_reduce_fusion.1 = (f32[9,16,128]{2,1,0:T(8,128)}, f32[9,16,128]{2,1,0:T(8,128)}, f32[9,16,128]{2,1,0:T(8,128)}, f32[9,8,16,128]{3,2,1,0:T(8,128)S(1)}) fusion(f32[9,8,16,128]{3,2,1,0:T(8,128)S(1)} %fusion.25, f32[9,8]{1,0:T(8,128)S(1)} %broadcast_multiply_fusion.13, f32[9,8,16,128]{3,2,1,0:T(8,128)S(1)} %copy-done.1, ...), kind=kLoop, calls=%fused_computation.79 | loop fusion | flops 4663296 | bytes 7709248 | tf_op jit(solution)/shard_map/reduce_sum | solution.py:90
  102.4 1.3 collective-permute-start.17
  103.7 3.4 %collective-permute-start.18 = (f32[9,1,16,128]{3,2,1,0:T(8,128)S(1)}, f32[9,1,16,128]{3,2,1,0:T(8,128)S(1)}, u32[]{:S(2)}, u32[]{:S(2)}) collective-permute-start(f32[9,1,16,128]{3,2,1,0:T(8,128)S(1)} %get-tuple-element.43), channel_id=1, source_target_pairs={{1,0},{3,2},{5,4},{7,6},{9,8},{11,10},{13,12},{15,14},{17,16},{19,... | collective-permute-start | bytes 221192 | tf_op jit(solution)/shard_map/ppermute | solution.py:17
  107.1 4.0 %psum.7 = f32[3,16,128]{2,1,0:T(8,128)} all-reduce(f32[3,16,128]{2,1,0:T(8,128)S(1)} %add_multiply_fusion.3), channel_id=1, replica_groups=mesh['lon'=16,'lat'=8,'lev'=2] {'lev'}, use_global_device_ids=true, to_apply=%region_6.7 | all-reduce | flops 6144 | bytes 49152 | tf_op jit(solution)/shard_map/psum | solution.py:146
  111.6 0.5 copy.117
  112.1 0.5 copy.118
  112.6 3.6 %collective-permute-start.20 = (f32[9,8,16,2]{2,1,3,0:T(8,128)S(1)}, f32[9,8,16,2]{2,1,3,0:T(8,128)}, u32[]{:S(2)}, u32[]{:S(2)}) collective-permute-start(f32[9,8,16,2]{2,1,3,0:T(8,128)S(1)} %copy.118), channel_id=1, source_target_pairs={{16,0},{32,16},{48,32},{64,48},{80,64},{96,80},{112,96},{128,112},... | collective-permute-start | bytes 27656 | tf_op jit(solution)/shard_map/ppermute | solution.py:17
  116.3 3.0 %collective-permute-start.21 = (f32[9,8,2,128]{3,1,2,0:T(8,128)S(1)}, f32[9,8,2,128]{3,1,2,0:T(8,128)S(1)}, u32[]{:S(2)}, u32[]{:S(2)}) collective-permute-start(f32[9,8,2,128]{3,1,2,0:T(8,128)S(1)} %copy.121), channel_id=1, source_target_pairs={{0,2},{2,4},{4,6},{6,8},{8,10},{10,12},{12,14},{1,3},{3,5},{5,7},{... | collective-permute-start | bytes 221192 | tf_op jit(solution)/shard_map/ppermute | solution.py:15
  119.4 4.7 %collective-permute-start.22 = (f32[9,8,2,128]{3,1,2,0:T(8,128)S(1)}, f32[9,8,2,128]{3,1,2,0:T(8,128)S(1)}, u32[]{:S(2)}, u32[]{:S(2)}) collective-permute-start(f32[9,8,2,128]{3,1,2,0:T(8,128)S(1)} %copy.122), channel_id=1, source_target_pairs={{2,0},{4,2},{6,4},{8,6},{10,8},{12,10},{14,12},{3,1},{5,3},{7,5},{... | collective-permute-start | bytes 221192 | tf_op jit(solution)/shard_map/ppermute | solution.py:17
  124.0 0.5 copy.119
  124.5 1.4 %copy.120 = f32[9,8,16,2]{3,2,1,0:T(8,128)S(1)} copy(f32[9,8,16,2]{2,1,3,0:T(8,128)} %collective-permute-done.20) | data formatting | bytes 18432 | tf_op jit(solution)/shard_map/ppermute | solution.py:17
  125.9 0.5 pad_maximum_fusion.2
  127.2 0.6 copy-done.4
  128.0 1.6 %fusion.7 = f32[9,8,16,128]{3,2,1,0:T(8,128)} fusion(f32[9,8,19,128]{3,2,1,0:T(8,128)S(1)} %get-tuple-element.30, f32[9,8,19,128]{3,2,1,0:T(8,128)S(1)} %get-tuple-element.29, f32[9,8,16,131]{3,2,1,0:T(8,128)S(1)} %get-tuple-element.24, f32[9,8,16,131]{3,2,1,0:T(8,128)S(1)} %get-tuple-element.23, f32[8,16,128]{2,1,0:T(8,128)S(1)} %broadcast_select_fusion, ...), kind=kLoop, calls=%fused_computation.23 | loop fusion | flops 3833856 | bytes 6308128 | tf_op jit(solution)/shard_map/add | solution.py:142
  (154 shorter events, 7.3 us)
Async XLA Ops:
  0.6 16.6 %copy-start = (f32[8,9]{1,0:T(8,128)S(1)}, f32[8,9]{1,0:T(8,128)}, u32[]{:S(2)}) copy-start(f32[8,9]{1,0:T(8,128)} %param.16) | copy-start | bytes 868
  1.4 1.5 %copy-start.29 = (f32[8]{0:T(128)}, f32[8]{0:T(128)S(1)}, u32[]{:S(2)}) copy-start(f32[8]{0:T(128)S(1)} %get-tuple-element.70) | copy-start | bytes 100
  1.4 1.7 %copy-start.27 = (f32[8]{0:T(128)}, f32[8]{0:T(128)S(1)}, u32[]{:S(2)}) copy-start(f32[8]{0:T(128)S(1)} %get-tuple-element.69) | copy-start | bytes 100
  1.4 1.6 %copy-start.25 = (f32[8]{0:T(128)}, f32[8]{0:T(128)S(1)}, u32[]{:S(2)}) copy-start(f32[8]{0:T(128)S(1)} %get-tuple-element.76) | copy-start | bytes 100
  1.4 2.0 %copy-start.23 = (f32[8]{0:T(128)}, f32[8]{0:T(128)S(1)}, u32[]{:S(2)}) copy-start(f32[8]{0:T(128)S(1)} %get-tuple-element.75) | copy-start | bytes 100
  1.5 1.4 %copy-start.1 = (f32[9,8,16,128]{3,2,1,0:T(8,128)S(1)}, f32[9,8,16,128]{3,2,1,0:T(8,128)}, u32[]{:S(2)}) copy-start(f32[9,8,16,128]{3,2,1,0:T(8,128)} %param.11) | copy-start | bytes 1769476
  3.6 5.1 %copy-start.8 = (f32[8,16,128]{2,1,0:T(8,128)S(1)}, f32[8,16,128]{2,1,0:T(8,128)}, u32[]{:S(2)}) copy-start(f32[8,16,128]{2,1,0:T(8,128)} %param.14) | copy-start | bytes 196612
  3.6 6.6 %copy-start.20 = (f32[2,8,16,128]{3,2,1,0:T(8,128)S(1)}, f32[2,8,16,128]{3,2,1,0:T(8,128)}, u32[]{:S(2)}) copy-start(f32[2,8,16,128]{3,2,1,0:T(8,128)} %param.13) | copy-start | bytes 393220
  3.6 13.6 %copy-start.21 = (s32[16,128]{1,0:T(8,128)S(1)}, s32[16,128]{1,0:T(8,128)}, u32[]{:S(2)}) copy-start(s32[16,128]{1,0:T(8,128)} %param.20) | copy-start | bytes 24580
  3.6 13.6 %copy-start.34 = (s32[16]{0:T(128)S(1)}, s32[16]{0:T(128)}, u32[]{:S(2)}) copy-start(s32[16]{0:T(128)} %param.17) | copy-start | bytes 196
  3.7 13.9 %copy-start.35 = (f32[16]{0:T(128)S(1)}, f32[16]{0:T(128)}, u32[]{:S(2)}) copy-start(f32[16]{0:T(128)} %param.18) | copy-start | bytes 196
  4.4 26.6 %collective-permute-start.1 = (f32[9,1,16,128]{3,2,1,0:T(8,128)}, f32[9,1,16,128]{3,2,1,0:T(8,128)S(1)}, u32[]{:S(2)}, u32[]{:S(2)}) collective-permute-start(f32[9,1,16,128]{3,2,1,0:T(8,128)} %get-tuple-element.54), channel_id=1, source_target_pairs={{0,1},{2,3},{4,5},{6,7},{8,9},{10,11},{12,13},{14,15},{16,17},{18,... | collective-permute-start | bytes 221192 | tf_op jit(solution)/shard_map/ppermute | solution.py:15
  5.7 25.3 %collective-permute-start.2 = (f32[9,1,16,128]{3,2,1,0:T(8,128)}, f32[9,1,16,128]{3,2,1,0:T(8,128)S(1)}, u32[]{:S(2)}, u32[]{:S(2)}) collective-permute-start(f32[9,1,16,128]{3,2,1,0:T(8,128)} %get-tuple-element.55), channel_id=1, source_target_pairs={{1,0},{3,2},{5,4},{7,6},{9,8},{11,10},{13,12},{15,14},{17,16},{19,... | collective-permute-start | bytes 221192 | tf_op jit(solution)/shard_map/ppermute | solution.py:17
  8.8 8.4 %copy-start.31 = (pred[8]{0:T(512)(128)(4,1)}, pred[8]{0:T(512)(128)(4,1)S(1)}, u32[]{:S(2)}) copy-start(pred[8]{0:T(512)(128)(4,1)S(1)} %fusion.46) | copy-start | bytes 28
  8.9 18.7 %collective-permute-start = (f32[1,1,16,128]{3,2,1,0:T(8,128)S(1)}, f32[1,1,16,128]{3,2,1,0:T(8,128)S(1)}, u32[]{:S(2)}, u32[]{:S(2)}) collective-permute-start(f32[1,1,16,128]{3,2,1,0:T(8,128)S(1)} %slice.569), channel_id=1, source_target_pairs={{0,1},{2,3},{4,5},{6,7},{8,9},{10,11},{12,13},{14,15},{16,17},{18,... | collective-permute-start | bytes 24584 | tf_op jit(solution)/shard_map/ppermute | solution.py:15
  10.4 9.4 %collective-permute-start.3 = (f32[2,8,16,2]{3,2,1,0:T(8,128)S(1)}, f32[2,8,16,2]{3,2,1,0:T(8,128)S(1)}, u32[]{:S(2)}, u32[]{:S(2)}) collective-permute-start(f32[2,8,16,2]{3,2,1,0:T(8,128)S(1)} %get-tuple-element.60), channel_id=1, source_target_pairs={{0,16},{16,32},{32,48},{48,64},{64,80},{80,96},{96,112},{112,128},... | collective-permute-start | bytes 6152 | tf_op jit(solution)/shard_map/ppermute | solution.py:15
  11.7 12.5 %collective-permute-start.4 = (f32[2,8,16,2]{3,2,1,0:T(8,128)S(1)}, f32[2,8,16,2]{3,2,1,0:T(8,128)S(1)}, u32[]{:S(2)}, u32[]{:S(2)}) collective-permute-start(f32[2,8,16,2]{3,2,1,0:T(8,128)S(1)} %get-tuple-element.61), channel_id=1, source_target_pairs={{16,0},{32,16},{48,32},{64,48},{80,64},{96,80},{112,96},{128,112},... | collective-permute-start | bytes 6152 | tf_op jit(solution)/shard_map/ppermute | solution.py:17
  19.7 8.6 %collective-permute-start.7 = (f32[2,8,2,128]{3,2,1,0:T(2,128)S(1)}, f32[2,8,2,128]{3,2,1,0:T(2,128)S(1)}, u32[]{:S(2)}, u32[]{:S(2)}) collective-permute-start(f32[2,8,2,128]{3,2,1,0:T(2,128)S(1)} %get-tuple-element.62), channel_id=1, source_target_pairs={{0,2},{2,4},{4,6},{6,8},{8,10},{10,12},{12,14},{1,3},{3,5},{5,7},{... | collective-permute-start | bytes 49160 | tf_op jit(solution)/shard_map/ppermute | solution.py:15
  24.3 6.0 %collective-permute-start.8 = (f32[2,8,2,128]{3,2,1,0:T(2,128)S(1)}, f32[2,8,2,128]{3,2,1,0:T(2,128)S(1)}, u32[]{:S(2)}, u32[]{:S(2)}) collective-permute-start(f32[2,8,2,128]{3,2,1,0:T(2,128)S(1)} %get-tuple-element.63), channel_id=1, source_target_pairs={{2,0},{4,2},{6,4},{8,6},{10,8},{12,10},{14,12},{3,1},{5,3},{7,5},{... | collective-permute-start | bytes 49160 | tf_op jit(solution)/shard_map/ppermute | solution.py:17
  31.0 0.6 copy-start.16
  31.0 0.7 copy-start.18
  36.2 14.8 %collective-permute-start.5 = (f32[9,8,16,2]{2,1,3,0:T(8,128)}, f32[9,8,16,2]{2,1,3,0:T(8,128)}, u32[]{:S(2)}, u32[]{:S(2)}) collective-permute-start(f32[9,8,16,2]{2,1,3,0:T(8,128)} %copy.101), channel_id=1, source_target_pairs={{0,16},{16,32},{32,48},{48,64},{64,80},{80,96},{96,112},{112,128},... | collective-permute-start | bytes 27656 | tf_op jit(solution)/shard_map/ppermute | solution.py:15
  38.3 14.8 %collective-permute-start.6 = (f32[9,8,16,2]{2,1,3,0:T(8,128)}, f32[9,8,16,2]{2,1,3,0:T(8,128)}, u32[]{:S(2)}, u32[]{:S(2)}) collective-permute-start(f32[9,8,16,2]{2,1,3,0:T(8,128)} %copy.102), channel_id=1, source_target_pairs={{16,0},{32,16},{48,32},{64,48},{80,64},{96,80},{112,96},{128,112},... | collective-permute-start | bytes 27656 | tf_op jit(solution)/shard_map/ppermute | solution.py:17
  42.6 15.0 %collective-permute-start.9 = (f32[9,8,2,128]{3,1,2,0:T(8,128)}, f32[9,8,2,128]{3,1,2,0:T(8,128)}, u32[]{:S(2)}, u32[]{:S(2)}) collective-permute-start(f32[9,8,2,128]{3,1,2,0:T(8,128)} %copy.105), channel_id=1, source_target_pairs={{0,2},{2,4},{4,6},{6,8},{8,10},{10,12},{12,14},{1,3},{3,5},{5,7},{... | collective-permute-start | bytes 221192 | tf_op jit(solution)/shard_map/ppermute | solution.py:15
  47.0 11.5 %collective-permute-start.10 = (f32[9,8,2,128]{3,1,2,0:T(8,128)}, f32[9,8,2,128]{3,1,2,0:T(8,128)}, u32[]{:S(2)}, u32[]{:S(2)}) collective-permute-start(f32[9,8,2,128]{3,1,2,0:T(8,128)} %copy.106), channel_id=1, source_target_pairs={{2,0},{4,2},{6,4},{8,6},{10,8},{12,10},{14,12},{3,1},{5,3},{7,5},{... | collective-permute-start | bytes 221192 | tf_op jit(solution)/shard_map/ppermute | solution.py:17
  57.6 2.1 %copy-start.2 = (f32[8,19,128]{2,1,0:T(8,128)S(1)}, f32[8,19,128]{2,1,0:T(8,128)}, u32[]{:S(2)}) copy-start(f32[8,19,128]{2,1,0:T(8,128)} %get-tuple-element.58) | copy-start | bytes 233476
  57.6 2.1 %copy-start.5 = (f32[8,19,128]{2,1,0:T(8,128)S(1)}, f32[8,19,128]{2,1,0:T(8,128)}, u32[]{:S(2)}) copy-start(f32[8,19,128]{2,1,0:T(8,128)} %get-tuple-element.59) | copy-start | bytes 233476
  59.7 0.9 copy-start.17
  59.7 0.9 copy-start.19
  60.6 0.8 copy-start.30
  60.6 1.0 copy-start.28
  61.4 0.7 copy-start.26
  61.6 0.7 copy-start.24
  62.3 7.9 %copy-start.32 = (f32[9]{0:T(128)S(1)}, f32[9]{0:T(128)}, u32[]{:S(2)}) copy-start(f32[9]{0:T(128)} %param.19) | copy-start | bytes 112
  62.3 7.9 %copy-start.33 = (f32[8]{0:T(128)S(1)}, f32[8]{0:T(128)}, u32[]{:S(2)}) copy-start(f32[8]{0:T(128)} %dynamic_slice.11) | copy-start | bytes 100
  62.3 8.0 %copy-start.22 = (s32[16,128]{1,0:T(8,128)S(1)}, s32[16,128]{1,0:T(8,128)}, u32[]{:S(2)}) copy-start(s32[16,128]{1,0:T(8,128)} %param.21) | copy-start | bytes 24580
  62.5 7.8 %collective-permute-start.11 = (f32[9,1,16,128]{3,2,1,0:T(8,128)S(1)}, f32[9,1,16,128]{3,2,1,0:T(8,128)S(1)}, u32[]{:S(2)}, u32[]{:S(2)}) collective-permute-start(f32[9,1,16,128]{3,2,1,0:T(8,128)S(1)} %get-tuple-element.48), channel_id=1, source_target_pairs={{0,1},{2,3},{4,5},{6,7},{8,9},{10,11},{12,13},{14,15},{16,17},{18,... | collective-permute-start | bytes 221192 | tf_op jit(solution)/shard_map/ppermute | solution.py:15
  63.8 7.3 %collective-permute-start.12 = (f32[9,1,16,128]{3,2,1,0:T(8,128)S(1)}, f32[9,1,16,128]{3,2,1,0:T(8,128)S(1)}, u32[]{:S(2)}, u32[]{:S(2)}) collective-permute-start(f32[9,1,16,128]{3,2,1,0:T(8,128)S(1)} %get-tuple-element.49), channel_id=1, source_target_pairs={{1,0},{3,2},{5,4},{7,6},{9,8},{11,10},{13,12},{15,14},{17,16},{19,... | collective-permute-start | bytes 221192 | tf_op jit(solution)/shard_map/ppermute | solution.py:17
  70.3 2.2 %copy-start.9 = (f32[9,1,16,128]{3,2,1,0:T(8,128)}, f32[9,1,16,128]{3,2,1,0:T(8,128)S(1)}, u32[]{:S(2)}) copy-start(f32[9,1,16,128]{3,2,1,0:T(8,128)S(1)} %collective-permute-done.11) | copy-start | bytes 221188
  71.1 1.5 %copy-start.11 = (f32[9,1,16,128]{3,2,1,0:T(8,128)}, f32[9,1,16,128]{3,2,1,0:T(8,128)S(1)}, u32[]{:S(2)}) copy-start(f32[9,1,16,128]{3,2,1,0:T(8,128)S(1)} %collective-permute-done.12) | copy-start | bytes 221188
  74.7 15.0 %collective-permute-start.13 = (f32[9,8,16,2]{2,1,3,0:T(8,128)}, f32[9,8,16,2]{2,1,3,0:T(8,128)}, u32[]{:S(2)}, u32[]{:S(2)}) collective-permute-start(f32[9,8,16,2]{2,1,3,0:T(8,128)} %copy.109), channel_id=1, source_target_pairs={{0,16},{16,32},{32,48},{48,64},{64,80},{80,96},{96,112},{112,128},... | collective-permute-start | bytes 27656 | tf_op jit(solution)/shard_map/ppermute | solution.py:15
  76.9 15.0 %collective-permute-start.14 = (f32[9,8,16,2]{2,1,3,0:T(8,128)}, f32[9,8,16,2]{2,1,3,0:T(8,128)}, u32[]{:S(2)}, u32[]{:S(2)}) collective-permute-start(f32[9,8,16,2]{2,1,3,0:T(8,128)} %copy.110), channel_id=1, source_target_pairs={{16,0},{32,16},{48,32},{64,48},{80,64},{96,80},{112,96},{128,112},... | collective-permute-start | bytes 27656 | tf_op jit(solution)/shard_map/ppermute | solution.py:17
  81.2 15.2 %collective-permute-start.15 = (f32[9,8,2,128]{3,1,2,0:T(8,128)}, f32[9,8,2,128]{3,1,2,0:T(8,128)}, u32[]{:S(2)}, u32[]{:S(2)}) collective-permute-start(f32[9,8,2,128]{3,1,2,0:T(8,128)} %copy.113), channel_id=1, source_target_pairs={{0,2},{2,4},{4,6},{6,8},{8,10},{10,12},{12,14},{1,3},{3,5},{5,7},{... | collective-permute-start | bytes 221192 | tf_op jit(solution)/shard_map/ppermute | solution.py:15
  85.7 11.6 %collective-permute-start.16 = (f32[9,8,2,128]{3,1,2,0:T(8,128)}, f32[9,8,2,128]{3,1,2,0:T(8,128)}, u32[]{:S(2)}, u32[]{:S(2)}) collective-permute-start(f32[9,8,2,128]{3,1,2,0:T(8,128)} %copy.114), channel_id=1, source_target_pairs={{2,0},{4,2},{6,4},{8,6},{10,8},{12,10},{14,12},{3,1},{5,3},{7,5},{... | collective-permute-start | bytes 221192 | tf_op jit(solution)/shard_map/ppermute | solution.py:17
  96.3 2.1 %copy-start.3 = (f32[8,19,128]{2,1,0:T(8,128)S(1)}, f32[8,19,128]{2,1,0:T(8,128)}, u32[]{:S(2)}) copy-start(f32[8,19,128]{2,1,0:T(8,128)} %get-tuple-element.58) | copy-start | bytes 233476
  96.4 2.1 %copy-start.6 = (f32[8,19,128]{2,1,0:T(8,128)S(1)}, f32[8,19,128]{2,1,0:T(8,128)}, u32[]{:S(2)}) copy-start(f32[8,19,128]{2,1,0:T(8,128)} %get-tuple-element.59) | copy-start | bytes 233476
  98.4 0.9 copy-start.10
  98.5 0.9 copy-start.12
  101.3 0.9 copy-start.15
  101.3 0.9 copy-start.14
  101.3 0.9 copy-start.13
  102.4 8.7 %collective-permute-start.17 = (f32[9,1,16,128]{3,2,1,0:T(8,128)S(1)}, f32[9,1,16,128]{3,2,1,0:T(8,128)S(1)}, u32[]{:S(2)}, u32[]{:S(2)}) collective-permute-start(f32[9,1,16,128]{3,2,1,0:T(8,128)S(1)} %get-tuple-element.42), channel_id=1, source_target_pairs={{0,1},{2,3},{4,5},{6,7},{8,9},{10,11},{12,13},{14,15},{16,17},{18,... | collective-permute-start | bytes 221192 | tf_op jit(solution)/shard_map/ppermute | solution.py:15
  103.7 7.4 %collective-permute-start.18 = (f32[9,1,16,128]{3,2,1,0:T(8,128)S(1)}, f32[9,1,16,128]{3,2,1,0:T(8,128)S(1)}, u32[]{:S(2)}, u32[]{:S(2)}) collective-permute-start(f32[9,1,16,128]{3,2,1,0:T(8,128)S(1)} %get-tuple-element.43), channel_id=1, source_target_pairs={{1,0},{3,2},{5,4},{7,6},{9,8},{11,10},{13,12},{15,14},{17,16},{19,... | collective-permute-start | bytes 221192 | tf_op jit(solution)/shard_map/ppermute | solution.py:17
  112.1 12.0 %collective-permute-start.19 = (f32[9,8,16,2]{2,1,3,0:T(8,128)S(1)}, f32[9,8,16,2]{2,1,3,0:T(8,128)S(1)}, u32[]{:S(2)}, u32[]{:S(2)}) collective-permute-start(f32[9,8,16,2]{2,1,3,0:T(8,128)S(1)} %copy.117), channel_id=1, source_target_pairs={{0,16},{16,32},{32,48},{48,64},{64,80},{80,96},{96,112},{112,128},... | collective-permute-start | bytes 27656 | tf_op jit(solution)/shard_map/ppermute | solution.py:15
  112.6 11.9 %collective-permute-start.20 = (f32[9,8,16,2]{2,1,3,0:T(8,128)S(1)}, f32[9,8,16,2]{2,1,3,0:T(8,128)}, u32[]{:S(2)}, u32[]{:S(2)}) collective-permute-start(f32[9,8,16,2]{2,1,3,0:T(8,128)S(1)} %copy.118), channel_id=1, source_target_pairs={{16,0},{32,16},{48,32},{64,48},{80,64},{96,80},{112,96},{128,112},... | collective-permute-start | bytes 27656 | tf_op jit(solution)/shard_map/ppermute | solution.py:17
  116.3 10.6 %collective-permute-start.21 = (f32[9,8,2,128]{3,1,2,0:T(8,128)S(1)}, f32[9,8,2,128]{3,1,2,0:T(8,128)S(1)}, u32[]{:S(2)}, u32[]{:S(2)}) collective-permute-start(f32[9,8,2,128]{3,1,2,0:T(8,128)S(1)} %copy.121), channel_id=1, source_target_pairs={{0,2},{2,4},{4,6},{6,8},{8,10},{10,12},{12,14},{1,3},{3,5},{5,7},{... | collective-permute-start | bytes 221192 | tf_op jit(solution)/shard_map/ppermute | solution.py:15
  119.4 7.6 %collective-permute-start.22 = (f32[9,8,2,128]{3,1,2,0:T(8,128)S(1)}, f32[9,8,2,128]{3,1,2,0:T(8,128)S(1)}, u32[]{:S(2)}, u32[]{:S(2)}) collective-permute-start(f32[9,8,2,128]{3,1,2,0:T(8,128)S(1)} %copy.122), channel_id=1, source_target_pairs={{2,0},{4,2},{6,4},{8,6},{10,8},{12,10},{14,12},{3,1},{5,3},{7,5},{... | collective-permute-start | bytes 221192 | tf_op jit(solution)/shard_map/ppermute | solution.py:17
  126.9 0.9 copy-start.4
  126.9 0.9 copy-start.7
where the time goes:
time: 132 us; the launch traced here: 130 us
  starting transfers between devices  66.4 us (50%)
  local copies, waits for them, and re-layouts  35.3 us (27%)
  other arithmetic  17.8 us (13%)
  waiting for transfers between devices  4.2 us (3%)
  blocking collectives  4.01 us (3%)
  between operations  1.63 us (1%)
    ppermute x11, starting transfers between devices, with_halo(): lax.ppermute(head, axis, [((i + 1) % count, i) for i in range(ends)])  44.6 us
    ppermute x12, starting transfers between devices, with_halo(): lax.ppermute(tail, axis, [(i, (i + 1) % count) for i in range(ends)])  21.8 us
    slice x16, local copies, waits for them, and re-layouts, with_halo(): lax.slice_in_dim(cells, cells.shape[dim] - width, cells.shape[dim], axis=...  9.57 us
    ppermute x6, local copies, waits for them, and re-layouts, with_halo(): lax.ppermute(head, axis, [((i + 1) % count, i) for i in range(ends)])  7.63 us
    ppermute x6, local copies, waits for them, and re-layouts, with_halo(): lax.ppermute(tail, axis, [(i, (i + 1) % count) for i in range(ends)])  6.89 us
    slice x6, local copies, waits for them, and re-layouts, with_halo(): head = lax.slice_in_dim(cells, 0, width, axis=dim)  6.14 us
    concatenate x6, other arithmetic, with_halo(): jnp.concatenate([lax.ppermute(tail, axis, [(i, (i + 1) % count) for i in...  4.52 us
    psum x1, blocking collectives, run_split(): emis_grad = lax.psum(emis_grad, 'lev')  4.01 us
  transfers between devices with their start and end apart: 23, of which 3 were waited for; matrix products, arithmetic and copies ran while one was open for 22% of the time, Pallas kernels for 0%

commit v1 on v0

v1 whole, which is shorter than its diff:
```python
import functools

import jax
import jax.numpy as jnp
from jax import lax
from jax.experimental import pallas as pl
from jax.experimental.pallas import tpu as pltpu
from jax.sharding import PartitionSpec as P

MESH = pl.DeviceIdType.MESH
PAD = 8


def with_halo(cells, axis, dim, lo, hi, closed):
    count = lax.axis_size(axis)
    ends = count if closed else count - 1
    parts = []
    if lo:
        tail = lax.slice_in_dim(cells, cells.shape[dim] - lo, cells.shape[dim], axis=dim)
        parts.append(lax.ppermute(tail, axis, [(i, (i + 1) % count) for i in range(ends)]))
    parts.append(cells)
    if hi:
        head = lax.slice_in_dim(cells, 0, hi, axis=dim)
        parts.append(lax.ppermute(head, axis, [((i + 1) % count, i) for i in range(ends)]))
    return jnp.concatenate(parts, axis=dim)


def face_weights(c_pad, dim, length):
    def at(shift):
        return lax.slice_in_dim(c_pad, 2 + shift, 2 + shift + length, axis=dim)

    return jnp.stack(
        [
            -1.5 * jnp.maximum(at(0), 0.0),
            0.5 * jnp.maximum(at(1), 0.0),
            -1.5 * jnp.minimum(at(-1), 0.0),
            0.5 * jnp.minimum(at(-2), 0.0),
        ]
    )


def kernel(
    adj_ref, traj_ref, cx_ref, cy_ref, vc_ref, src_ref, scal_ref,
    out_ref, emis_ref,
    pad_ref, at_ref, ht_ref, hb_ref, lv_ref, eo_ref, ep_ref, send_sem, recv_sem,
):
    n_t, n_z, n_y, n_x = adj_ref.shape
    steps = traj_ref.shape[0]
    rows = n_z * n_y
    lon = lax.axis_index("lon")
    lat = lax.axis_index("lat")
    lev = lax.axis_index("lev")
    n_lon = lax.axis_size("lon")
    n_lat = lax.axis_size("lat")
    right = lax.rem(lon + 1, n_lon)
    left = lax.rem(lon + n_lon - 1, n_lon)
    has_up = lat < n_lat - 1
    has_down = lat > 0
    up = jnp.minimum(lat + 1, n_lat - 1)
    down = jnp.maximum(lat - 1, 0)
    partner = 1 - lev
    edge_z = jnp.where(lev == 0, n_z - 1, 0)

    zeros_pad = jnp.zeros((n_t, n_z, PAD, n_x), jnp.float32)
    for k in range(steps):
        pad_ref[k, :, :, 0:PAD, :] = zeros_pad
        pad_ref[k, :, :, PAD + n_y : 2 * PAD + n_y, :] = zeros_pad

    barrier = pltpu.get_barrier_semaphore()
    for dev in ((lon, lat, partner), (left, lat, lev), (right, lat, lev)):
        pl.semaphore_signal(barrier, 1, device_id=dev, device_id_type=MESH)

    @pl.when(has_up)
    def _():
        pl.semaphore_signal(barrier, 1, device_id=(lon, up, lev), device_id_type=MESH)

    @pl.when(has_down)
    def _():
        pl.semaphore_signal(barrier, 1, device_id=(lon, down, lev), device_id_type=MESH)

    pl.semaphore_wait(barrier, 3 + has_up.astype(jnp.int32) + has_down.astype(jnp.int32))

    off_rate = 0
    off_speed = 6 * n_z
    off_emis = off_speed + n_t * n_z

    def rcopy(src, dst, idx, dev):
        return pltpu.make_async_remote_copy(
            src, dst, send_sem.at[idx], recv_sem.at[idx], device_id=dev, device_id_type=MESH
        )

    eo_ref[...] = jnp.zeros(eo_ref.shape, jnp.float32)
    src_mask = src_ref[...]
    lane = lax.broadcasted_iota(jnp.int32, (n_y, n_x), 1)

    for k in range(steps - 1, -1, -1):
        cur = adj_ref if k == steps - 1 else out_ref

        def coag_body(z, acc):
            lam = [cur[t, z] for t in range(n_t)]
            st = [traj_ref[k, t, z].astype(jnp.float32) for t in range(n_t)]
            new_acc = []
            for m in range(3):
                part = acc[m]
                for j in range(3):
                    part = part + scal_ref[off_emis + (3 * m + j) * n_z + z] * lam[3 * m + j]
                new_acc.append(part)
            kr = [scal_ref[off_rate + i * n_z + z] for i in range(6)]
            k0, k1, k2, k01, k02, k12 = kr
            n0, v0, w0, n1, v1, w1, n2, v2, w2 = st
            ln0, lv0, lw0, ln1, lv1, lw1, ln2, lv2, lw2 = lam
            a01 = k01 * n1
            a02 = k02 * n2
            a12 = k12 * n2
            s0 = a01 + a02
            g_n0 = ln0 * (-2.0 * k0 * n0 - s0)
            g_v0 = (
                (lv1 * a01 + lv2 * a02 - lv0 * s0)
                + 2.0 * (lw0 * (k0 * v0) + lw1 * (k01 * v1) + lw2 * (k02 * v2))
            )
            g_w0 = lw1 * a01 + lw2 * a02 - lw0 * s0
            g_n1 = (
                ln1 * (-2.0 * k1 * n1 - a12)
                - ln0 * (k01 * n0)
                + (lv1 - lv0) * (k01 * v0)
                + (lw1 - lw0) * (k01 * w0)
            )
            g_v1 = (lv2 - lv1) * a12 + 2.0 * (lw1 * (k1 * v1 + k01 * v0) + lw2 * (k12 * v2))
            g_w1 = (lw2 - lw1) * a12
            g_n2 = (
                -2.0 * k2 * n2 * ln2
                - ln0 * (k02 * n0)
                - ln1 * (k12 * n1)
                + (lv2 - lv0) * (k02 * v0)
                + (lv2 - lv1) * (k12 * v1)
                + (lw2 - lw0) * (k02 * w0)
                + (lw2 - lw1) * (k12 * w1)
            )
            g_v2 = 2.0 * lw2 * (k2 * v2 + k02 * v0 + k12 * v1)
            grads = [g_n0, g_v0, g_w0, g_n1, g_v1, g_w1, g_n2, g_v2, None]
            for t in range(n_t):
                if grads[t] is None:
                    out_ref[t, z] = lam[t]
                else:
                    out_ref[t, z] = lam[t] + grads[t]
            return tuple(new_acc)

        zero = jnp.zeros((n_y, n_x), jnp.float32)
        acc = lax.fori_loop(0, n_z, coag_body, (zero, zero, zero))
        for m in range(3):
            eo_ref[m] = eo_ref[m] + acc[m] * src_mask

        lev_copy = rcopy(
            out_ref.at[:, pl.ds(edge_z, 1)], lv_ref.at[k], k, (lon, lat, partner)
        )
        lev_copy.start()
        lev_copy.wait()

        below_ok = lev == 1
        above_ok = lev == 0

        def vert_body(i, carry):
            t = i // n_z
            z = i % n_z
            a = out_ref[t, z]
            halo = lv_ref[k, t, 0]
            a_below = jnp.where(z > 0, out_ref[t, jnp.maximum(z - 1, 0)], jnp.where(below_ok, halo, 0.0))
            a_above = jnp.where(z < n_z - 1, out_ref[t, jnp.minimum(z + 1, n_z - 1)], jnp.where(above_ok, halo, 0.0))
            s = scal_ref[off_speed + t * n_z + z]
            m_above = vc_ref[0, z]
            m_below = vc_ref[1, z]
            base = vc_ref[2, z]
            pad_ref[k, t, z, PAD : PAD + n_y, :] = (
                a * (base - s) + a_below * (m_below + s) + a_above * m_above
            )
            return carry

        lax.fori_loop(0, n_t * n_z, vert_body, 0)

        lat_up = rcopy(
            pad_ref.at[k, :, :, pl.ds(PAD + n_y - 2, 2), :],
            pad_ref.at[k, :, :, pl.ds(PAD - 2, 2), :],
            3 + k,
            (lon, up, lev),
        )
        lat_down = rcopy(
            pad_ref.at[k, :, :, pl.ds(PAD, 2), :],
            pad_ref.at[k, :, :, pl.ds(PAD + n_y, 2), :],
            6 + k,
            (lon, down, lev),
        )

        @pl.when(has_up)
        def _():
            lat_up.start()

        @pl.when(has_down)
        def _():
            lat_down.start()

        for t in range(n_t):
            blk = pad_ref[k, t, :, PAD : PAD + n_y, :].reshape(rows, n_x)
            at_ref[k, :, t * rows : (t + 1) * rows] = blk.T
        lon_right = rcopy(
            at_ref.at[k, pl.ds(n_x - 2, 2), :], ht_ref.at[k, pl.ds(n_x - 2, 2), :], 9 + k, (right, lat, lev)
        )
        lon_left = rcopy(
            at_ref.at[k, pl.ds(0, 2), :], ht_ref.at[k, pl.ds(0, 2), :], 12 + k, (left, lat, lev)
        )
        lon_right.start()
        lon_left.start()
        lon_right.wait()
        lon_left.wait()

        @pl.when(has_up)
        def _():
            lat_up.wait_send()
            lat_down.wait_recv()

        @pl.when(has_down)
        def _():
            lat_down.wait_send()
            lat_up.wait_recv()

        for t in range(n_t):
            hb_ref[t] = ht_ref[k, :, t * rows : (t + 1) * rows].T.reshape(n_z, n_y, n_x)

        def tr_body(i, carry):
            t = i // n_z
            z = i % n_z
            a = pad_ref[k, t, z, PAD : PAD + n_y, :]
            hz = hb_ref[t, z]
            y_p1 = pad_ref[k, t, z, PAD + 1 : PAD + 1 + n_y, :]
            y_p2 = pad_ref[k, t, z, PAD + 2 : PAD + 2 + n_y, :]
            y_m1 = pad_ref[k, t, z, PAD - 1 : PAD - 1 + n_y, :]
            y_m2 = pad_ref[k, t, z, PAD - 2 : PAD - 2 + n_y, :]
            x_p1 = jnp.where(lane == n_x - 1, pltpu.roll(hz, n_x - 1, 1), pltpu.roll(a, n_x - 1, 1))
            x_p2 = jnp.where(lane >= n_x - 2, pltpu.roll(hz, n_x - 2, 1), pltpu.roll(a, n_x - 2, 1))
            x_m1 = jnp.where(lane == 0, pltpu.roll(hz, 1, 1), pltpu.roll(a, 1, 1))
            x_m2 = jnp.where(lane <= 1, pltpu.roll(hz, 2, 1), pltpu.roll(a, 2, 1))
            lon_part = (
                cx_ref[0, z] * (a - x_p1)
                + cx_ref[1, z] * (x_p1 - x_p2)
                + cx_ref[2, z] * (x_m1 - a)
                + cx_ref[3, z] * (x_m2 - x_m1)
            )
            lat_part = (
                cy_ref[0, z] * (a - y_p1)
                + cy_ref[1, z] * (y_p1 - y_p2)
                + cy_ref[2, z] * (y_m1 - a)
                + cy_ref[3, z] * (y_m2 - y_m1)
            )
            out_ref[t, z] = a + lon_part + lat_part
            return carry

        lax.fori_loop(0, n_t * n_z, tr_body, 0)

    emis_copy = rcopy(eo_ref, ep_ref, 15, (lon, lat, partner))
    emis_copy.start()
    emis_copy.wait()
    emis_ref[...] = eo_ref[...] + ep_ref[...]


def shards(
    adjoint_in,
    trajectory,
    courant,
    mixing,
    coag_rates,
    settle_speed,
    settle_class,
    emis_profile,
    emis_coef,
    land_mask,
    source_mask,
):
    n_t, n_z, n_y, n_x = adjoint_in.shape
    lev_index = lax.axis_index("lev")
    lat_index = lax.axis_index("lat")
    lat_count = lax.axis_size("lat")
    level_total = settle_class.shape[0]
    level_start = lev_index * n_z
    level_global = level_start + jnp.arange(n_z, dtype=jnp.int32)
    row_global = lat_index * n_y + jnp.arange(n_y, dtype=jnp.int32)
    top_row = (row_global == n_y * lat_count - 1)[None, :, None]
    east = courant[0]
    north = jnp.where(top_row, 0.0, courant[1])
    east_pad = with_halo(east, "lon", 2, 2, 1, True)
    north_pad = with_halo(north, "lat", 1, 2, 1, False)
    cx = face_weights(east_pad, 2, n_x)
    cy = face_weights(north_pad, 1, n_y)

    mixing_top = jnp.where((level_global == level_total - 1)[:, None, None], 0.0, mixing)
    mixing_below = with_halo(mixing_top, "lev", 0, 1, 0, False)[:n_z]
    surface = (level_global == 0).astype(jnp.float32)
    deposit = (0.1 + 0.3 * land_mask.astype(jnp.float32))[None] * surface[:, None, None]
    base = 1.0 - mixing_top - mixing_below - deposit
    vc = jnp.stack([mixing_top, mixing_below, base])

    choose = (
        settle_class[:, None] == jnp.arange(settle_speed.shape[0], dtype=jnp.int32)[None, :]
    ).astype(jnp.float32)
    speeds_all = jnp.dot(choose, settle_speed, precision=lax.Precision.HIGHEST).T
    speeds_used = lax.dynamic_slice_in_dim(speeds_all, level_start, n_z, 1)
    rates_own = lax.dynamic_slice_in_dim(coag_rates, level_start, n_z, 1)
    profile_own = lax.dynamic_slice_in_dim(emis_profile, level_start, n_z, 0)
    emis_w = emis_coef[:, None] * profile_own[None, :]
    scal = jnp.concatenate([rates_own.reshape(-1), speeds_used.reshape(-1), emis_w.reshape(-1)])
    source = source_mask.astype(jnp.float32)
    steps = trajectory.shape[0]

    vmem = pl.BlockSpec(memory_space=pltpu.VMEM)
    smem = pl.BlockSpec(memory_space=pltpu.SMEM)
    return pl.pallas_call(
        kernel,
        out_shape=(
            jax.ShapeDtypeStruct(adjoint_in.shape, jnp.float32),
            jax.ShapeDtypeStruct((3, n_y, n_x), jnp.float32),
        ),
        in_specs=[vmem, vmem, vmem, vmem, vmem, vmem, smem],
        out_specs=(vmem, vmem),
        scratch_shapes=[
            pltpu.VMEM((steps, n_t, n_z, n_y + 2 * PAD, n_x), jnp.float32),
            pltpu.VMEM((steps, n_x, n_t * n_z * n_y), jnp.float32),
            pltpu.VMEM((steps, n_x, n_t * n_z * n_y), jnp.float32),
            pltpu.VMEM((n_t, n_z, n_y, n_x), jnp.float32),
            pltpu.VMEM((steps, n_t, 1, n_y, n_x), jnp.float32),
            pltpu.VMEM((3, n_y, n_x), jnp.float32),
            pltpu.VMEM((3, n_y, n_x), jnp.float32),
            pltpu.SemaphoreType.DMA((16,)),
            pltpu.SemaphoreType.DMA((16,)),
        ],
        compiler_params=pltpu.CompilerParams(
            collective_id=0, has_side_effects=True, vmem_limit_bytes=48 * 1024 * 1024
        ),
    )(adjoint_in, trajectory, cx, cy, vc, source, scal)


def solution(mesh):
    return jax.shard_map(
        shards,
        mesh=mesh,
        in_specs=(
            P(None, "lev", "lat", "lon"),
            P(None, None, "lev", "lat", "lon"),
            P(None, "lev", "lat", "lon"),
            P("lev", "lat", "lon"),
            P(),
            P(),
            P(),
            P(),
            P(),
            P("lat", "lon"),
            P("lat", "lon"),
        ),
        out_specs=(P(None, "lev", "lat", "lon"), P(None, "lat", "lon")),
        check_vma=False,
    )
```

time: 132 us -> 79 us (0.60); the launches traced: 130 us -> 78.7 us
  Pallas kernels: 0 us -> 55.1 us
  starting transfers between devices: 66.4 us -> 14.8 us
  local copies, waits for them, and re-layouts: 35.3 us -> 6.02 us
  other arithmetic: 17.8 us -> 1.71 us
  waiting for transfers between devices: 4.2 us -> 0.01 us
  blocking collectives: 4.01 us -> 0 us
    pallas_call x0 -> x1, Pallas kernels: none -> 55.1 us  [shards(): pl.pallas_call(kernel, out_shape=(jax.ShapeDtypeStruct(adjoint_in.shape,...]
    ppermute x11 -> x2, starting transfers between devices: 44.6 us -> 10.2 us  [with_halo(): lax.ppermute(head, axis, [((i + 1) % count, i) for i in range(ends)])]
    ppermute x12 -> x3, starting transfers between devices: 21.8 us -> 4.63 us  [with_halo(): lax.ppermute(tail, axis, [(i, (i + 1) % count) for i in range(ends)])]
    slice x22 -> x4, local copies, waits for them, and re-layouts: 15.7 us -> 0.09 us  [the longest x3 0.09 us: with_halo(): lax.slice_in_dim(cells, cells.shape[dim] - lo, cells.shape[dim], axis=dim)]
    ppermute x12 -> x0, local copies, waits for them, and re-layouts: 14.5 us -> none  [the longest x6 7.63 us: with_halo(): lax.ppermute(head, axis, [((i + 1) % count, i) for i in range(ends)])]
    concatenate x6 -> x1, other arithmetic: 4.52 us -> 0.08 us  [shards(): jnp.concatenate([rates_own.reshape(-1), speeds_used.reshape(-1), emis_w.r...]
    add x10 -> x1, other arithmetic: 4.14 us -> 0.01 us  [shards(): 0.1 + 0.3 * land_mask.astype(jnp.float32)]
    psum x1 -> x0, blocking collectives: 4.01 us -> none  [run_split(): emis_grad = lax.psum(emis_grad, 'lev')]
  transfers between devices with their start and end apart: 23 -> 5, of which waited for: 3 -> 0; matrix products, arithmetic and copies ran while one was open for 22% -> 2% of each run, Pallas kernels for 0% -> 0%
where the time goes in v1:
time: 79 us; the launch traced here: 78.7 us
  Pallas kernels  55.1 us (70%)
  starting transfers between devices  14.8 us (19%)
  local copies, waits for them, and re-layouts  6.02 us (8%)
  other arithmetic  1.71 us (2%)
  between operations  0.84 us (1%)
    pallas_call x1, Pallas kernels, shards(): pl.pallas_call(kernel, out_shape=(jax.ShapeDtypeStruct(adjoint_in.shape,...  55.1 us
    ppermute x2, starting transfers between devices, with_halo(): lax.ppermute(head, axis, [((i + 1) % count, i) for i in range(ends)])  10.2 us
    unnamed x24, local copies, waits for them, and re-layouts  5.46 us
    ppermute x3, starting transfers between devices, with_halo(): lax.ppermute(tail, axis, [(i, (i + 1) % count) for i in range(ends)])  4.63 us
  transfers between devices with their start and end apart: 5, of which 0 were waited for; matrix products, arithmetic and copies ran while one was open for 2% of the time, Pallas kernels for 0%

profile of v1, /device:TPU:5, one launch (start us, length us, event | category | flops | bytes accessed | tf_op | source)
XLA Modules:
  0.0 78.7 jit_solution(11461045536499513400)
XLA Ops:
  0.6 0.0 copy-start
  0.7 0.0 copy-start.4
  0.7 0.0 copy-start.3
  0.7 1.0 %bitcast_select_fusion = f32[8,16,128]{2,1,0:T(8,128)S(1)} fusion(f32[2,8,16,128]{3,2,1,0:T(8,128)} %param.13, pred[16]{0:T(512)(128)(4,1)S(1)} %add_compare_fusion), kind=kLoop, calls=%fused_computation.32 | loop fusion | flops 16384 | bytes 131088 | tf_op jit(solution)/shard_map/jit(_where)/select_n | solution.py:287
  1.7 4.8 %collective-permute-start.2 = (f32[8,1,128]{2,1,0:T(1,128)S(1)}, f32[8,1,128]{2,1,0:T(1,128)S(1)}, u32[]{:S(2)}, u32[]{:S(2)}) collective-permute-start(f32[8,1,128]{2,1,0:T(1,128)S(1)} %slice.66), channel_id=1, source_target_pairs={{2,0},{4,2},{6,4},{8,6},{10,8},{12,10},{14,12},{3,1},{5,3},{7,5},{... | collective-permute-start | bytes 12296 | tf_op jit(solution)/shard_map/ppermute | solution.py:24
  6.5 2.0 %collective-permute-start.3 = (f32[8,2,128]{2,1,0:T(2,128)S(1)}, f32[8,2,128]{2,1,0:T(2,128)S(1)}, u32[]{:S(2)}, u32[]{:S(2)}) collective-permute-start(f32[8,2,128]{2,1,0:T(2,128)S(1)} %slice.67), channel_id=1, source_target_pairs={{0,2},{2,4},{4,6},{6,8},{8,10},{10,12},{12,14},{1,3},{3,5},{5,7},{... | collective-permute-start | bytes 24584 | tf_op jit(solution)/shard_map/ppermute | solution.py:20
  8.5 0.0 copy-done.4
  8.5 0.1 broadcast_select_fusion
  8.6 1.3 %collective-permute-start.4 = (f32[1,16,128]{2,1,0:T(8,128)S(1)}, f32[1,16,128]{2,1,0:T(8,128)S(1)}, u32[]{:S(2)}, u32[]{:S(2)}) collective-permute-start(f32[1,16,128]{2,1,0:T(8,128)S(1)} %slice.70), channel_id=1, source_target_pairs={{0,1},{2,3},{4,5},{6,7},{8,9},{10,11},{12,13},{14,15},{16,17},{18,... | collective-permute-start | bytes 24584 | tf_op jit(solution)/shard_map/ppermute | solution.py:20
  9.9 0.0 copy-done.3
  9.9 0.1 maximum_multiply_fusion
  10.0 0.1 slice.63
  10.1 1.3 %collective-permute-start.1 = (f32[8,16,2]{2,1,0:T(8,128)S(1)}, f32[8,16,2]{2,1,0:T(8,128)S(1)}, u32[]{:S(2)}, u32[]{:S(2)}) collective-permute-start(f32[8,16,2]{2,1,0:T(8,128)S(1)} %slice.63), channel_id=1, source_target_pairs={{0,16},{16,32},{32,48},{48,64},{64,80},{80,96},{96,112},{112,128},... | collective-permute-start | bytes 3080 | tf_op jit(solution)/shard_map/ppermute | solution.py:20
  11.4 5.4 %collective-permute-start = (f32[8,16,1]{2,1,0:T(8,128)S(1)}, f32[8,16,1]{2,1,0:T(8,128)S(1)}, u32[]{:S(2)}, u32[]{:S(2)}) collective-permute-start(f32[8,16,1]{2,1,0:T(8,128)S(1)} %bitcast.26), channel_id=1, source_target_pairs={{16,0},{32,16},{48,32},{64,48},{80,64},{96,80},{112,96},{128,112},... | collective-permute-start | bytes 1544 | tf_op jit(solution)/shard_map/ppermute | solution.py:24
  16.8 0.0 copy-start.9
  16.8 0.1 fusion.25
  16.9 0.0 copy-start.7
  16.9 0.6 copy-done.9
  17.5 0.1 dynamic_slice.11
  17.5 0.0 copy-done.7
  17.6 0.1 constant_dynamic-slice_fusion
  17.6 0.0 copy-start.8
  17.6 0.1 reshape.32
  17.7 0.6 copy-done.8
  18.3 0.1 broadcast_multiply_fusion
  18.4 0.0 copy-start.10
  18.4 0.1 mul.86
  18.4 0.0 copy-done
  18.5 0.6 copy-done.10
  19.0 0.2 fusion.21
  19.2 0.0 copy-start.5
  19.2 0.1 copy.14
  19.3 0.1 reshape.33
  19.4 0.5 copy-done.5
  19.9 0.0 copy-start.6
  19.9 0.1 pad_maximum_fusion.8.scal_ref
  20.0 0.6 copy-done.6
  20.6 0.0 collective-permute-done
  20.6 0.0 collective-permute-done.1
  20.6 0.2 fusion.7
  20.8 0.0 copy-start.1
  20.8 0.0 collective-permute-done.4
  20.8 0.1 fusion.20
  20.9 0.0 copy-start.2
  20.9 0.0 collective-permute-done.2
  21.0 0.0 collective-permute-done.3
  21.0 0.9 %copy-done.1 = bf16[3,9,8,16,128]{4,3,2,1,0:T(8,128)(2,1)S(1)} copy-done((bf16[3,9,8,16,128]{4,3,2,1,0:T(8,128)(2,1)S(1)}, bf16[3,9,8,16,128]{4,3,2,1,0:T(8,128)(2,1)}, u32[]{:S(2)}) %copy-start.1) | copy-done | bytes 884760
  22.0 0.2 copy-done.2
  22.1 55.1 %shard_map.122 = (f32[9,8,16,128]{3,2,1,0:T(8,128)S(1)}, f32[3,16,128]{2,1,0:T(8,128)S(1)}) custom-call(f32[9,8,16,128]{3,2,1,0:T(8,128)S(1)} %copy-done.2, bf16[3,9,8,16,128]{4,3,2,1,0:T(8,128)(2,1)S(1)} %copy-done.1, f32[4,8,16,128]{3,2,1,0:T(8,128)S(1)} %pad_maximum_fusion.cx_ref, f32[4,8,16,128]{3,2,1,0:T(8,128)S(1)} %pad_maximum_fusion.1.cy_ref, ...), custom_call_target="tpu_custom_call" | custom-call | tf_op jit(solution)/shard_map/pallas_call | solution.py:314
  77.2 0.8 %copy.17 = f32[9,8,16,128]{3,2,1,0:T(8,128)} copy(f32[9,8,16,128]{3,2,1,0:T(8,128)S(1)} %get-tuple-element.15) | data formatting | bytes 1179648
  78.1 0.6 copy.18
  (13 shorter events, 0.1 us)
Async XLA Ops:
  0.6 17.8 %copy-start = (f32[8,9]{1,0:T(8,128)S(1)}, f32[8,9]{1,0:T(8,128)}, u32[]{:S(2)}) copy-start(f32[8,9]{1,0:T(8,128)} %param.16) | copy-start | bytes 868
  0.7 7.9 %copy-start.4 = (f32[8,16,128]{2,1,0:T(8,128)S(1)}, f32[8,16,128]{2,1,0:T(8,128)}, u32[]{:S(2)}) copy-start(f32[8,16,128]{2,1,0:T(8,128)} %param.14) | copy-start | bytes 196612
  0.7 9.2 %copy-start.3 = (f32[2,8,16,128]{3,2,1,0:T(8,128)S(1)}, f32[2,8,16,128]{3,2,1,0:T(8,128)}, u32[]{:S(2)}) copy-start(f32[2,8,16,128]{3,2,1,0:T(8,128)} %param.13) | copy-start | bytes 393220
  1.7 19.3 %collective-permute-start.2 = (f32[8,1,128]{2,1,0:T(1,128)S(1)}, f32[8,1,128]{2,1,0:T(1,128)S(1)}, u32[]{:S(2)}, u32[]{:S(2)}) collective-permute-start(f32[8,1,128]{2,1,0:T(1,128)S(1)} %slice.66), channel_id=1, source_target_pairs={{2,0},{4,2},{6,4},{8,6},{10,8},{12,10},{14,12},{3,1},{5,3},{7,5},{... | collective-permute-start | bytes 12296 | tf_op jit(solution)/shard_map/ppermute | solution.py:24
  6.5 14.5 %collective-permute-start.3 = (f32[8,2,128]{2,1,0:T(2,128)S(1)}, f32[8,2,128]{2,1,0:T(2,128)S(1)}, u32[]{:S(2)}, u32[]{:S(2)}) collective-permute-start(f32[8,2,128]{2,1,0:T(2,128)S(1)} %slice.67), channel_id=1, source_target_pairs={{0,2},{2,4},{4,6},{6,8},{8,10},{10,12},{12,14},{1,3},{3,5},{5,7},{... | collective-permute-start | bytes 24584 | tf_op jit(solution)/shard_map/ppermute | solution.py:20
  8.6 12.2 %collective-permute-start.4 = (f32[1,16,128]{2,1,0:T(8,128)S(1)}, f32[1,16,128]{2,1,0:T(8,128)S(1)}, u32[]{:S(2)}, u32[]{:S(2)}) collective-permute-start(f32[1,16,128]{2,1,0:T(8,128)S(1)} %slice.70), channel_id=1, source_target_pairs={{0,1},{2,3},{4,5},{6,7},{8,9},{10,11},{12,13},{14,15},{16,17},{18,... | collective-permute-start | bytes 24584 | tf_op jit(solution)/shard_map/ppermute | solution.py:20
  10.1 10.6 %collective-permute-start.1 = (f32[8,16,2]{2,1,0:T(8,128)S(1)}, f32[8,16,2]{2,1,0:T(8,128)S(1)}, u32[]{:S(2)}, u32[]{:S(2)}) collective-permute-start(f32[8,16,2]{2,1,0:T(8,128)S(1)} %slice.63), channel_id=1, source_target_pairs={{0,16},{16,32},{32,48},{48,64},{64,80},{80,96},{96,112},{112,128},... | collective-permute-start | bytes 3080 | tf_op jit(solution)/shard_map/ppermute | solution.py:20
  11.4 9.2 %collective-permute-start = (f32[8,16,1]{2,1,0:T(8,128)S(1)}, f32[8,16,1]{2,1,0:T(8,128)S(1)}, u32[]{:S(2)}, u32[]{:S(2)}) collective-permute-start(f32[8,16,1]{2,1,0:T(8,128)S(1)} %bitcast.26), channel_id=1, source_target_pairs={{16,0},{32,16},{48,32},{64,48},{80,64},{96,80},{112,96},{128,112},... | collective-permute-start | bytes 1544 | tf_op jit(solution)/shard_map/ppermute | solution.py:24
  16.8 0.7 copy-start.9
  16.9 0.7 copy-start.7
  17.6 0.7 copy-start.8
  18.4 0.7 copy-start.10
  19.2 0.7 copy-start.5
  19.9 0.7 copy-start.6
  20.8 1.2 %copy-start.1 = (bf16[3,9,8,16,128]{4,3,2,1,0:T(8,128)(2,1)S(1)}, bf16[3,9,8,16,128]{4,3,2,1,0:T(8,128)(2,1)}, u32[]{:S(2)}) copy-start(bf16[3,9,8,16,128]{4,3,2,1,0:T(8,128)(2,1)} %traj_ref.1) | copy-start | bytes 2654212
  20.9 1.2 %copy-start.2 = (f32[9,8,16,128]{3,2,1,0:T(8,128)S(1)}, f32[9,8,16,128]{3,2,1,0:T(8,128)}, u32[]{:S(2)}) copy-start(f32[9,8,16,128]{3,2,1,0:T(8,128)} %adj_ref.1) | copy-start | bytes 1769476

commit v2 on v1

v2 whole, which is shorter than its diff:
```python
import jax
import jax.numpy as jnp
from jax import lax
from jax.experimental import pallas as pl
from jax.experimental.pallas import tpu as pltpu
from jax.sharding import PartitionSpec as P

MESH = pl.DeviceIdType.MESH
PAD = 8

S_LEV, S_UP, S_DOWN, S_RIGHT, S_LEFT = 0, 3, 6, 9, 12
S_EMIS, S_CE_R, S_CE_L, S_CN_U, S_CN_D, S_MIX = 15, 16, 17, 18, 19, 20
N_REMOTE = 21


def kernel(
    adj_hbm, traj_hbm, cour_hbm, mix_hbm, land_ref, srcm_ref,
    rates_ref, speed_ref, sclass_ref, prof_ref, ecoef_ref,
    out_ref, emis_ref,
    traj_ref, cour_ref, mix_ref, pad_ref, at_ref, ht_ref, hb_ref, lv_ref, eo_ref, ep_ref,
    cx_ref, cy_ref, vc_ref, cet_ref, ceh_ref, cyp_ref, mh_ref,
    send_sem, recv_sem, local_sem,
):
    n_t, n_z, n_y, n_x = out_ref.shape
    steps = traj_hbm.shape[0]
    rows = n_z * n_y
    lon = lax.axis_index("lon")
    lat = lax.axis_index("lat")
    lev = lax.axis_index("lev")
    n_lon = lax.axis_size("lon")
    n_lat = lax.axis_size("lat")
    right = lax.rem(lon + 1, n_lon)
    left = lax.rem(lon + n_lon - 1, n_lon)
    has_up = lat < n_lat - 1
    has_down = lat > 0
    up = jnp.minimum(lat + 1, n_lat - 1)
    down = jnp.maximum(lat - 1, 0)
    partner = 1 - lev
    low_half = lev == 0
    edge_z = jnp.where(low_half, n_z - 1, 0)
    inner_z = jnp.where(low_half, n_z - 2, 1)
    level0 = lev * n_z

    adj_in = pltpu.make_async_copy(adj_hbm, out_ref, local_sem.at[0])
    cour_in = pltpu.make_async_copy(cour_hbm, cour_ref, local_sem.at[1])
    mix_in = pltpu.make_async_copy(mix_hbm, mix_ref, local_sem.at[2])
    traj_in = [
        pltpu.make_async_copy(traj_hbm.at[k], traj_ref.at[k], local_sem.at[3 + k]) for k in range(steps)
    ]
    cour_in.start()
    mix_in.start()
    adj_in.start()
    for k in range(steps - 1, -1, -1):
        traj_in[k].start()

    zeros_pad = jnp.zeros((n_t, n_z, PAD, n_x), jnp.float32)
    for k in range(steps):
        pad_ref[k, :, :, 0:PAD, :] = zeros_pad
        pad_ref[k, :, :, PAD + n_y : 2 * PAD + n_y, :] = zeros_pad
    zeros_c = jnp.zeros((n_z, PAD, n_x), jnp.float32)
    cyp_ref[:, 0:PAD, :] = zeros_c
    cyp_ref[:, PAD + n_y : 2 * PAD + n_y, :] = zeros_c

    barrier = pltpu.get_barrier_semaphore()
    for dev in ((lon, lat, partner), (left, lat, lev), (right, lat, lev)):
        pl.semaphore_signal(barrier, 1, device_id=dev, device_id_type=MESH)

    @pl.when(has_up)
    def _():
        pl.semaphore_signal(barrier, 1, device_id=(lon, up, lev), device_id_type=MESH)

    @pl.when(has_down)
    def _():
        pl.semaphore_signal(barrier, 1, device_id=(lon, down, lev), device_id_type=MESH)

    pl.semaphore_wait(barrier, 3 + has_up.astype(jnp.int32) + has_down.astype(jnp.int32))

    def rcopy(src, dst, idx, dev):
        return pltpu.make_async_remote_copy(
            src, dst, send_sem.at[idx], recv_sem.at[idx], device_id=dev, device_id_type=MESH
        )

    lane = lax.broadcasted_iota(jnp.int32, (n_y, n_x), 1)
    row = lax.broadcasted_iota(jnp.int32, (n_y, n_x), 0)

    cour_in.wait()
    mix_in.wait()
    top_row = jnp.logical_and(lat == n_lat - 1, row == n_y - 1)
    for z in range(n_z):
        cyp_ref[z, PAD : PAD + n_y, :] = jnp.where(top_row, 0.0, cour_ref[1, z])
    cet_ref[...] = cour_ref[0].reshape(rows, n_x).T
    ce_right = rcopy(cet_ref.at[pl.ds(n_x - 2, 2), :], ceh_ref.at[pl.ds(n_x - 2, 2), :], S_CE_R, (right, lat, lev))
    ce_left = rcopy(cet_ref.at[pl.ds(0, 2), :], ceh_ref.at[pl.ds(0, 2), :], S_CE_L, (left, lat, lev))
    cn_up = rcopy(
        cyp_ref.at[:, pl.ds(PAD + n_y - 2, 2), :], cyp_ref.at[:, pl.ds(PAD - 2, 2), :], S_CN_U, (lon, up, lev)
    )
    cn_down = rcopy(
        cyp_ref.at[:, pl.ds(PAD, 2), :], cyp_ref.at[:, pl.ds(PAD + n_y, 2), :], S_CN_D, (lon, down, lev)
    )
    mix_x = rcopy(mix_ref.at[pl.ds(edge_z, 1)], mh_ref, S_MIX, (lon, lat, partner))
    mix_x.start()
    ce_right.start()
    ce_left.start()

    @pl.when(has_up)
    def _():
        cn_up.start()

    @pl.when(has_down)
    def _():
        cn_down.start()

    def build_vertical_coefficients():
        mix_x.wait()
        dep = jnp.where(low_half, 0.1 + 0.3 * land_ref[...].astype(jnp.float32), 0.0)
        below = jnp.where(low_half, 0.0, mh_ref[0])
        for z in range(n_z):
            above = mix_ref[z]
            if z == n_z - 1:
                above = jnp.where(low_half, above, 0.0)
            base = 1.0 - above - below
            if z == 0:
                base = base - dep
            vc_ref[0, z] = above
            vc_ref[1, z] = below
            vc_ref[2, z] = base
            below = above

    def build_transport_coefficients():
        ce_right.wait()
        ce_left.wait()

        @pl.when(has_up)
        def _():
            cn_up.wait_send()
            cn_down.wait_recv()

        @pl.when(has_down)
        def _():
            cn_down.wait_send()
            cn_up.wait_recv()

        he = ceh_ref[...].T.reshape(n_z, n_y, n_x)
        for z in range(n_z):
            c = cour_ref[0, z]
            hz = he[z]
            c_p1 = jnp.where(lane == n_x - 1, pltpu.roll(hz, n_x - 1, 1), pltpu.roll(c, n_x - 1, 1))
            c_m1 = jnp.where(lane == 0, pltpu.roll(hz, 1, 1), pltpu.roll(c, 1, 1))
            c_m2 = jnp.where(lane <= 1, pltpu.roll(hz, 2, 1), pltpu.roll(c, 2, 1))
            cx_ref[0, z] = -1.5 * jnp.maximum(c, 0.0)
            cx_ref[1, z] = 0.5 * jnp.maximum(c_p1, 0.0)
            cx_ref[2, z] = -1.5 * jnp.minimum(c_m1, 0.0)
            cx_ref[3, z] = 0.5 * jnp.minimum(c_m2, 0.0)
            cy_ref[0, z] = -1.5 * jnp.maximum(cyp_ref[z, PAD : PAD + n_y, :], 0.0)
            cy_ref[1, z] = 0.5 * jnp.maximum(cyp_ref[z, PAD + 1 : PAD + 1 + n_y, :], 0.0)
            cy_ref[2, z] = -1.5 * jnp.minimum(cyp_ref[z, PAD - 1 : PAD - 1 + n_y, :], 0.0)
            cy_ref[3, z] = 0.5 * jnp.minimum(cyp_ref[z, PAD - 2 : PAD - 2 + n_y, :], 0.0)

    eo_ref[...] = jnp.zeros(eo_ref.shape, jnp.float32)
    src_mask = srcm_ref[...].astype(jnp.float32)
    adj_in.wait()

    for k in range(steps - 1, -1, -1):
        traj_in[k].wait()

        def coag_level(zz, acc):
            z = jnp.where(low_half, n_z - 1 - zz, zz)
            zg = level0 + z
            lam = [out_ref[t, z] for t in range(n_t)]
            st = [traj_ref[k, t, z].astype(jnp.float32) for t in range(n_t)]
            new_acc = []
            for m in range(3):
                part = acc[m]
                for j in range(3):
                    part = part + (ecoef_ref[3 * m + j] * prof_ref[zg]) * lam[3 * m + j]
                new_acc.append(part)
            k0, k1, k2, k01, k02, k12 = [rates_ref[i, zg] for i in range(6)]
            n0, v0, w0, n1, v1, w1, n2, v2, w2 = st
            ln0, lv0, lw0, ln1, lv1, lw1, ln2, lv2, lw2 = lam
            a01 = k01 * n1
            a02 = k02 * n2
            a12 = k12 * n2
            s0 = a01 + a02
            g_n0 = ln0 * (-2.0 * k0 * n0 - s0)
            g_v0 = (
                (lv1 * a01 + lv2 * a02 - lv0 * s0)
                + 2.0 * (lw0 * (k0 * v0) + lw1 * (k01 * v1) + lw2 * (k02 * v2))
            )
            g_w0 = lw1 * a01 + lw2 * a02 - lw0 * s0
            g_n1 = (
                ln1 * (-2.0 * k1 * n1 - a12)
                - ln0 * (k01 * n0)
                + (lv1 - lv0) * (k01 * v0)
                + (lw1 - lw0) * (k01 * w0)
            )
            g_v1 = (lv2 - lv1) * a12 + 2.0 * (lw1 * (k1 * v1 + k01 * v0) + lw2 * (k12 * v2))
            g_w1 = (lw2 - lw1) * a12
            g_n2 = (
                -2.0 * k2 * n2 * ln2
                - ln0 * (k02 * n0)
                - ln1 * (k12 * n1)
                + (lv2 - lv0) * (k02 * v0)
                + (lv2 - lv1) * (k12 * v1)
                + (lw2 - lw0) * (k02 * w0)
                + (lw2 - lw1) * (k12 * w1)
            )
            g_v2 = 2.0 * lw2 * (k2 * v2 + k02 * v0 + k12 * v1)
            grads = [g_n0, g_v0, g_w0, g_n1, g_v1, g_w1, g_n2, g_v2]
            for t in range(n_t - 1):
                out_ref[t, z] = lam[t] + grads[t]
            return tuple(new_acc)

        zero = jnp.zeros((n_y, n_x), jnp.float32)
        acc = coag_level(0, (zero, zero, zero))
        lev_copy = rcopy(out_ref.at[:, pl.ds(edge_z, 1)], lv_ref.at[k], S_LEV + k, (lon, lat, partner))
        lev_copy.start()
        acc = lax.fori_loop(1, n_z, coag_level, acc)
        for m in range(3):
            eo_ref[m] = eo_ref[m] + acc[m] * src_mask

        if k == steps - 1:
            build_vertical_coefficients()

        def vert_inner(i, carry):
            t = i // (n_z - 1)
            z = i % (n_z - 1) + lev
            zg = level0 + z
            s = speed_ref[sclass_ref[zg], t]
            a = out_ref[t, z]
            a_below = jnp.where(z > 0, out_ref[t, jnp.maximum(z - 1, 0)], 0.0)
            a_above = jnp.where(z < n_z - 1, out_ref[t, jnp.minimum(z + 1, n_z - 1)], 0.0)
            pad_ref[k, t, z, PAD : PAD + n_y, :] = (
                a * (vc_ref[2, z] - s) + a_below * (vc_ref[1, z] + s) + a_above * vc_ref[0, z]
            )
            return carry

        lax.fori_loop(0, n_t * (n_z - 1), vert_inner, 0, unroll=7)
        lev_copy.wait()

        def vert_edge(t, carry):
            z = edge_z
            s = speed_ref[sclass_ref[level0 + z], t]
            a = out_ref[t, z]
            other = out_ref[t, inner_z]
            halo = lv_ref[k, t, 0]
            a_below = jnp.where(low_half, other, halo)
            a_above = jnp.where(low_half, halo, other)
            pad_ref[k, t, z, PAD : PAD + n_y, :] = (
                a * (vc_ref[2, z] - s) + a_below * (vc_ref[1, z] + s) + a_above * vc_ref[0, z]
            )
            return carry

        lax.fori_loop(0, n_t, vert_edge, 0, unroll=3)

        lat_up = rcopy(
            pad_ref.at[k, :, :, pl.ds(PAD + n_y - 2, 2), :],
            pad_ref.at[k, :, :, pl.ds(PAD - 2, 2), :],
            S_UP + k,
            (lon, up, lev),
        )
        lat_down = rcopy(
            pad_ref.at[k, :, :, pl.ds(PAD, 2), :],
            pad_ref.at[k, :, :, pl.ds(PAD + n_y, 2), :],
            S_DOWN + k,
            (lon, down, lev),
        )

        @pl.when(has_up)
        def _():
            lat_up.start()

        @pl.when(has_down)
        def _():
            lat_down.start()

        for t in range(n_t):
            blk = pad_ref[k, t, :, PAD : PAD + n_y, :].reshape(rows, n_x)
            at_ref[k, :, t * rows : (t + 1) * rows] = blk.T
        lon_right = rcopy(
            at_ref.at[k, pl.ds(n_x - 2, 2), :], ht_ref.at[k, pl.ds(n_x - 2, 2), :], S_RIGHT + k, (right, lat, lev)
        )
        lon_left = rcopy(
            at_ref.at[k, pl.ds(0, 2), :], ht_ref.at[k, pl.ds(0, 2), :], S_LEFT + k, (left, lat, lev)
        )
        lon_right.start()
        lon_left.start()

        if k == steps - 1:
            build_transport_coefficients()

        lon_right.wait()
        lon_left.wait()

        @pl.when(has_up)
        def _():
            lat_up.wait_send()
            lat_down.wait_recv()

        @pl.when(has_down)
        def _():
            lat_down.wait_send()
            lat_up.wait_recv()

        for t in range(n_t):
            hb_ref[t] = ht_ref[k, :, t * rows : (t + 1) * rows].T.reshape(n_z, n_y, n_x)

        def transport(i, carry):
            t = i // n_z
            z = i % n_z
            a = pad_ref[k, t, z, PAD : PAD + n_y, :]
            hz = hb_ref[t, z]
            y_p1 = pad_ref[k, t, z, PAD + 1 : PAD + 1 + n_y, :]
            y_p2 = pad_ref[k, t, z, PAD + 2 : PAD + 2 + n_y, :]
            y_m1 = pad_ref[k, t, z, PAD - 1 : PAD - 1 + n_y, :]
            y_m2 = pad_ref[k, t, z, PAD - 2 : PAD - 2 + n_y, :]
            x_p1 = jnp.where(lane == n_x - 1, pltpu.roll(hz, n_x - 1, 1), pltpu.roll(a, n_x - 1, 1))
            x_p2 = jnp.where(lane >= n_x - 2, pltpu.roll(hz, n_x - 2, 1), pltpu.roll(a, n_x - 2, 1))
            x_m1 = jnp.where(lane == 0, pltpu.roll(hz, 1, 1), pltpu.roll(a, 1, 1))
            x_m2 = jnp.where(lane <= 1, pltpu.roll(hz, 2, 1), pltpu.roll(a, 2, 1))
            lon_part = (
                cx_ref[0, z] * (a - x_p1)
                + cx_ref[1, z] * (x_p1 - x_p2)
                + cx_ref[2, z] * (x_m1 - a)
                + cx_ref[3, z] * (x_m2 - x_m1)
            )
            lat_part = (
                cy_ref[0, z] * (a - y_p1)
                + cy_ref[1, z] * (y_p1 - y_p2)
                + cy_ref[2, z] * (y_m1 - a)
                + cy_ref[3, z] * (y_m2 - y_m1)
            )
            out_ref[t, z] = a + lon_part + lat_part
            return carry

        lax.fori_loop(0, n_t * n_z, transport, 0, unroll=4)

    emis_copy = rcopy(eo_ref, ep_ref, S_EMIS, (lon, lat, partner))
    emis_copy.start()
    emis_copy.wait()
    emis_ref[...] = eo_ref[...] + ep_ref[...]


def shards(
    adjoint_in,
    trajectory,
    courant,
    mixing,
    coag_rates,
    settle_speed,
    settle_class,
    emis_profile,
    emis_coef,
    land_mask,
    source_mask,
):
    n_t, n_z, n_y, n_x = adjoint_in.shape
    steps = trajectory.shape[0]
    rows = n_z * n_y
    hbm = pl.BlockSpec(memory_space=pl.ANY)
    vmem = pl.BlockSpec(memory_space=pltpu.VMEM)
    smem = pl.BlockSpec(memory_space=pltpu.SMEM)
    f32 = jnp.float32
    return pl.pallas_call(
        kernel,
        out_shape=(
            jax.ShapeDtypeStruct(adjoint_in.shape, f32),
            jax.ShapeDtypeStruct((3, n_y, n_x), f32),
        ),
        in_specs=[hbm, hbm, hbm, hbm, vmem, vmem, smem, smem, smem, smem, smem],
        out_specs=(vmem, vmem),
        scratch_shapes=[
            pltpu.VMEM(trajectory.shape, trajectory.dtype),
            pltpu.VMEM(courant.shape, f32),
            pltpu.VMEM(mixing.shape, f32),
            pltpu.VMEM((steps, n_t, n_z, n_y + 2 * PAD, n_x), f32),
            pltpu.VMEM((steps, n_x, n_t * rows), f32),
            pltpu.VMEM((steps, n_x, n_t * rows), f32),
            pltpu.VMEM((n_t, n_z, n_y, n_x), f32),
            pltpu.VMEM((steps, n_t, 1, n_y, n_x), f32),
            pltpu.VMEM((3, n_y, n_x), f32),
            pltpu.VMEM((3, n_y, n_x), f32),
            pltpu.VMEM((4, n_z, n_y, n_x), f32),
            pltpu.VMEM((4, n_z, n_y, n_x), f32),
            pltpu.VMEM((3, n_z, n_y, n_x), f32),
            pltpu.VMEM((n_x, rows), f32),
            pltpu.VMEM((n_x, rows), f32),
            pltpu.VMEM((n_z, n_y + 2 * PAD, n_x), f32),
            pltpu.VMEM((1, n_y, n_x), f32),
            pltpu.SemaphoreType.DMA((N_REMOTE,)),
            pltpu.SemaphoreType.DMA((N_REMOTE,)),
            pltpu.SemaphoreType.DMA((3 + steps,)),
        ],
        compiler_params=pltpu.CompilerParams(
            collective_id=0, has_side_effects=True, vmem_limit_bytes=48 * 1024 * 1024
        ),
    )(
        adjoint_in, trajectory, courant, mixing, land_mask, source_mask,
        coag_rates, settle_speed, settle_class, emis_profile, emis_coef,
    )


def solution(mesh):
    return jax.shard_map(
        shards,
        mesh=mesh,
        in_specs=(
            P(None, "lev", "lat", "lon"),
            P(None, None, "lev", "lat", "lon"),
            P(None, "lev", "lat", "lon"),
            P("lev", "lat", "lon"),
            P(),
            P(),
            P(),
            P(),
            P(),
            P("lat", "lon"),
            P("lat", "lon"),
        ),
        out_specs=(P(None, "lev", "lat", "lon"), P(None, "lat", "lon")),
        check_vma=False,
    )
```

time: 79 us -> 53.7 us (0.68)
  starting transfers between devices: 14.8 us -> 0 us
  Pallas kernels: 55.1 us -> 42.5 us
  local copies, waits for them, and re-layouts: 6.02 us -> 10.1 us
  other arithmetic: 1.71 us -> 0 us
    ppermute x5 -> x0, starting transfers between devices: 14.8 us -> none  [the longest x2 10.2 us: with_halo(): lax.ppermute(head, axis, [((i + 1) % count, i) for i in range(ends)])]
    pallas_call x1, Pallas kernels: 55.1 us -> 42.5 us  [shards(): pl.pallas_call(kernel, out_shape=(jax.ShapeDtypeStruct(adjoint_in.shape,...]
    unnamed x24, local copies, waits for them, and re-layouts: 5.46 us -> 10.1 us
    select_n x2 -> x0, other arithmetic: 1.05 us -> none  [the longest x1 0.98 us: shards(): north = jnp.where(top_row, 0.0, courant[1])]
  transfers between devices with their start and end apart: 5 -> 0, of which waited for: 0 -> 0; matrix products, arithmetic and copies ran while one was open for 2% -> 0% of each run, Pallas kernels for 0% -> 0%
where the time goes in v2:
time: 53.7 us; the launch traced here: 53.3 us
  Pallas kernels  42.5 us (79%)
  local copies, waits for them, and re-layouts  10.1 us (19%)
  between operations  0.66 us (1%)
    pallas_call x1, Pallas kernels, shards(): pl.pallas_call(kernel, out_shape=(jax.ShapeDtypeStruct(adjoint_in.shape,...  42.5 us
    unnamed x24, local copies, waits for them, and re-layouts  10.1 us

profile of v2, /device:TPU:5, one launch (start us, length us, event | category | flops | bytes accessed | tf_op | source)
XLA Modules:
  0.0 53.3 jit_solution(10325875940954154745)
XLA Ops:
  0.6 0.0 copy-start
  0.6 1.2 %copy-done = bf16[3,9,8,16,128]{4,3,2,1,0:T(8,128)(2,1)S(1)} copy-done((bf16[3,9,8,16,128]{4,3,2,1,0:T(8,128)(2,1)S(1)}, bf16[3,9,8,16,128]{4,3,2,1,0:T(8,128)(2,1)}, u32[]{:S(2)}) %copy-start) | copy-done | bytes 884760
  1.8 0.0 copy-start.1
  1.8 1.1 %copy-done.1 = f32[9,8,16,128]{3,2,1,0:T(8,128)S(1)} copy-done((f32[9,8,16,128]{3,2,1,0:T(8,128)S(1)}, f32[9,8,16,128]{3,2,1,0:T(8,128)}, u32[]{:S(2)}) %copy-start.1) | copy-done | bytes 589848
  2.9 0.0 copy-start.2
  2.9 0.9 %copy-done.2 = f32[2,8,16,128]{3,2,1,0:T(8,128)S(1)} copy-done((f32[2,8,16,128]{3,2,1,0:T(8,128)S(1)}, f32[2,8,16,128]{3,2,1,0:T(8,128)}, u32[]{:S(2)}) %copy-start.2) | copy-done | bytes 131096
  3.8 0.0 copy-start.3
  3.8 0.8 %copy-done.3 = f32[8,16,128]{2,1,0:T(8,128)S(1)} copy-done((f32[8,16,128]{2,1,0:T(8,128)S(1)}, f32[8,16,128]{2,1,0:T(8,128)}, u32[]{:S(2)}) %copy-start.3) | copy-done | bytes 65560
  4.6 0.0 copy-start.4
  4.6 0.7 %copy-done.4 = s32[16,128]{1,0:T(8,128)S(1)} copy-done((s32[16,128]{1,0:T(8,128)S(1)}, s32[16,128]{1,0:T(8,128)}, u32[]{:S(2)}) %copy-start.4) | copy-done | bytes 8216
  5.3 0.0 copy-start.5
  5.3 0.7 %copy-done.5 = s32[16,128]{1,0:T(8,128)S(1)} copy-done((s32[16,128]{1,0:T(8,128)S(1)}, s32[16,128]{1,0:T(8,128)}, u32[]{:S(2)}) %copy-start.5) | copy-done | bytes 8216
  6.0 0.0 copy-start.6
  6.0 0.7 %copy-done.6 = f32[6,16]{1,0:T(8,128)S(1)} copy-done((f32[6,16]{1,0:T(8,128)S(1)}, f32[6,16]{1,0:T(8,128)}, u32[]{:S(2)}) %copy-start.6) | copy-done | bytes 408
  6.7 0.0 copy-start.7
  6.7 0.7 %copy-done.7 = f32[8,9]{1,0:T(8,128)S(1)} copy-done((f32[8,9]{1,0:T(8,128)S(1)}, f32[8,9]{1,0:T(8,128)}, u32[]{:S(2)}) %copy-start.7) | copy-done | bytes 312
  7.4 0.0 copy-start.8
  7.4 0.7 %copy-done.8 = s32[16]{0:T(128)S(1)} copy-done((s32[16]{0:T(128)S(1)}, s32[16]{0:T(128)}, u32[]{:S(2)}) %copy-start.8) | copy-done | bytes 88
  8.0 0.0 copy-start.9
  8.0 0.7 %copy-done.9 = f32[16]{0:T(128)S(1)} copy-done((f32[16]{0:T(128)S(1)}, f32[16]{0:T(128)}, u32[]{:S(2)}) %copy-start.9) | copy-done | bytes 88
  8.7 0.0 copy-start.10
  8.7 0.7 %copy-done.10 = f32[9]{0:T(128)S(1)} copy-done((f32[9]{0:T(128)S(1)}, f32[9]{0:T(128)}, u32[]{:S(2)}) %copy-start.10) | copy-done | bytes 60
  9.3 42.5 %shard_map.122 = (f32[9,8,16,128]{3,2,1,0:T(8,128)S(1)}, f32[3,16,128]{2,1,0:T(8,128)S(1)}) custom-call(f32[9,8,16,128]{3,2,1,0:T(8,128)S(1)} %copy-done.1, bf16[3,9,8,16,128]{4,3,2,1,0:T(8,128)(2,1)S(1)} %copy-done, f32[2,8,16,128]{3,2,1,0:T(8,128)S(1)} %copy-done.2, f32[8,16,128]{2,1,0:T(8,128)S(1)} %copy-done.3, s32[16,128]{1,0:T(8,128)S(1)} %copy-done.4, ...), custom_call_target="tpu_custom_call" | custom-call | tf_op jit(solution)/shard_map/pallas_call | solution.py:363
  51.9 0.8 %copy.15 = f32[9,8,16,128]{3,2,1,0:T(8,128)} copy(f32[9,8,16,128]{3,2,1,0:T(8,128)S(1)} %get-tuple-element.4) | data formatting | bytes 1179648
  52.7 0.6 %copy.16 = f32[3,16,128]{2,1,0:T(8,128)} copy(f32[3,16,128]{2,1,0:T(8,128)S(1)} %get-tuple-element.5) | data formatting | bytes 49152
Async XLA Ops:
  0.6 1.2 %copy-start = (bf16[3,9,8,16,128]{4,3,2,1,0:T(8,128)(2,1)S(1)}, bf16[3,9,8,16,128]{4,3,2,1,0:T(8,128)(2,1)}, u32[]{:S(2)}) copy-start(bf16[3,9,8,16,128]{4,3,2,1,0:T(8,128)(2,1)} %traj_hbm.1) | copy-start | bytes 2654212
  1.8 1.1 %copy-start.1 = (f32[9,8,16,128]{3,2,1,0:T(8,128)S(1)}, f32[9,8,16,128]{3,2,1,0:T(8,128)}, u32[]{:S(2)}) copy-start(f32[9,8,16,128]{3,2,1,0:T(8,128)} %adj_hbm.1) | copy-start | bytes 1769476
  2.9 0.9 %copy-start.2 = (f32[2,8,16,128]{3,2,1,0:T(8,128)S(1)}, f32[2,8,16,128]{3,2,1,0:T(8,128)}, u32[]{:S(2)}) copy-start(f32[2,8,16,128]{3,2,1,0:T(8,128)} %cour_hbm.1) | copy-start | bytes 393220
  3.8 0.8 %copy-start.3 = (f32[8,16,128]{2,1,0:T(8,128)S(1)}, f32[8,16,128]{2,1,0:T(8,128)}, u32[]{:S(2)}) copy-start(f32[8,16,128]{2,1,0:T(8,128)} %mix_hbm.1) | copy-start | bytes 196612
  4.6 0.7 %copy-start.4 = (s32[16,128]{1,0:T(8,128)S(1)}, s32[16,128]{1,0:T(8,128)}, u32[]{:S(2)}) copy-start(s32[16,128]{1,0:T(8,128)} %land_ref.1) | copy-start | bytes 24580
  5.3 0.7 %copy-start.5 = (s32[16,128]{1,0:T(8,128)S(1)}, s32[16,128]{1,0:T(8,128)}, u32[]{:S(2)}) copy-start(s32[16,128]{1,0:T(8,128)} %srcm_ref.1) | copy-start | bytes 24580
  6.0 0.7 %copy-start.6 = (f32[6,16]{1,0:T(8,128)S(1)}, f32[6,16]{1,0:T(8,128)}, u32[]{:S(2)}) copy-start(f32[6,16]{1,0:T(8,128)} %rates_ref.1) | copy-start | bytes 1156
  6.7 0.7 %copy-start.7 = (f32[8,9]{1,0:T(8,128)S(1)}, f32[8,9]{1,0:T(8,128)}, u32[]{:S(2)}) copy-start(f32[8,9]{1,0:T(8,128)} %speed_ref.1) | copy-start | bytes 868
  7.4 0.7 %copy-start.8 = (s32[16]{0:T(128)S(1)}, s32[16]{0:T(128)}, u32[]{:S(2)}) copy-start(s32[16]{0:T(128)} %sclass_ref.1) | copy-start | bytes 196
  8.0 0.7 %copy-start.9 = (f32[16]{0:T(128)S(1)}, f32[16]{0:T(128)}, u32[]{:S(2)}) copy-start(f32[16]{0:T(128)} %prof_ref.1) | copy-start | bytes 196
  8.7 0.7 %copy-start.10 = (f32[9]{0:T(128)S(1)}, f32[9]{0:T(128)}, u32[]{:S(2)}) copy-start(f32[9]{0:T(128)} %ecoef_ref.1) | copy-start | bytes 112

commit v3 on v2

--- a/solution.py
+++ b/solution.py
@@ -14,9 +14,10 @@
 
 
 def kernel(
-    adj_hbm, traj_hbm, cour_hbm, mix_hbm, land_ref, srcm_ref,
-    rates_ref, speed_ref, sclass_ref, prof_ref, ecoef_ref,
-    out_ref, emis_ref,
+    adj_hbm, traj_hbm, cour_hbm, mix_hbm, land_hbm, srcm_hbm,
+    rates_hbm, speed_hbm, sclass_hbm, prof_hbm, ecoef_hbm,
+    out_hbm, emis_hbm,
+    out_ref, emis_ref, land_ref, srcm_ref, rates_ref, speed_ref, sclass_ref, prof_ref, ecoef_ref,
     traj_ref, cour_ref, mix_ref, pad_ref, at_ref, ht_ref, hb_ref, lv_ref, eo_ref, ep_ref,
     cx_ref, cy_ref, vc_ref, cet_ref, ceh_ref, cyp_ref, mh_ref,
     send_sem, recv_sem, local_sem,
@@ -47,6 +48,22 @@
     traj_in = [
         pltpu.make_async_copy(traj_hbm.at[k], traj_ref.at[k], local_sem.at[3 + k]) for k in range(steps)
     ]
+    small_in = [
+        pltpu.make_async_copy(src, dst, local_sem.at[3 + steps + i])
+        for i, (src, dst) in enumerate(
+            (
+                (rates_hbm, rates_ref),
+                (speed_hbm, speed_ref),
+                (sclass_hbm, sclass_ref),
+                (prof_hbm, prof_ref),
+                (ecoef_hbm, ecoef_ref),
+                (land_hbm, land_ref),
+                (srcm_hbm, srcm_ref),
+            )
+        )
+    ]
+    for c in small_in:
+        c.start()
     cour_in.start()
     mix_in.start()
     adj_in.start()
@@ -85,6 +102,8 @@
 
     cour_in.wait()
     mix_in.wait()
+    for c in small_in:
+        c.wait()
     top_row = jnp.logical_and(lat == n_lat - 1, row == n_y - 1)
     for z in range(n_z):
         cyp_ref[z, PAD : PAD + n_y, :] = jnp.where(top_row, 0.0, cour_ref[1, z])
@@ -338,6 +357,12 @@
     emis_copy.start()
     emis_copy.wait()
     emis_ref[...] = eo_ref[...] + ep_ref[...]
+    out_copy = pltpu.make_async_copy(out_ref, out_hbm, local_sem.at[0])
+    emis_out = pltpu.make_async_copy(emis_ref, emis_hbm, local_sem.at[1])
+    out_copy.start()
+    emis_out.start()
+    out_copy.wait()
+    emis_out.wait()
 
 
 def shards(
@@ -366,9 +391,18 @@
             jax.ShapeDtypeStruct(adjoint_in.shape, f32),
             jax.ShapeDtypeStruct((3, n_y, n_x), f32),
         ),
-        in_specs=[hbm, hbm, hbm, hbm, vmem, vmem, smem, smem, smem, smem, smem],
-        out_specs=(vmem, vmem),
+        in_specs=[hbm] * 11,
+        out_specs=(hbm, hbm),
         scratch_shapes=[
+            pltpu.VMEM(adjoint_in.shape, f32),
+            pltpu.VMEM((3, n_y, n_x), f32),
+            pltpu.VMEM(land_mask.shape, land_mask.dtype),
+            pltpu.VMEM(source_mask.shape, source_mask.dtype),
+            pltpu.SMEM(coag_rates.shape, f32),
+            pltpu.SMEM(settle_speed.shape, f32),
+            pltpu.SMEM(settle_class.shape, settle_class.dtype),
+            pltpu.SMEM(emis_profile.shape, f32),
+            pltpu.SMEM(emis_coef.shape, f32),
             pltpu.VMEM(trajectory.shape, trajectory.dtype),
             pltpu.VMEM(courant.shape, f32),
             pltpu.VMEM(mixing.shape, f32),
@@ -388,10 +422,10 @@
             pltpu.VMEM((1, n_y, n_x), f32),
             pltpu.SemaphoreType.DMA((N_REMOTE,)),
             pltpu.SemaphoreType.DMA((N_REMOTE,)),
-            pltpu.SemaphoreType.DMA((3 + steps,)),
+            pltpu.SemaphoreType.DMA((10 + steps,)),
         ],
         compiler_params=pltpu.CompilerParams(
-            collective_id=0, has_side_effects=True, vmem_limit_bytes=48 * 1024 * 1024
+            collective_id=0, has_side_effects=True, vmem_limit_bytes=67043328
         ),
     )(
         adjoint_in, trajectory, courant, mixing, land_mask, source_mask,

time: 53.7 us -> 45.6 us (0.85)
  local copies, waits for them, and re-layouts: 10.1 us -> 2.53 us
    unnamed x24 -> x4, local copies, waits for them, and re-layouts: 10.1 us -> 2.53 us
where the time goes in v3:
time: 45.6 us; the launch traced here: 45.5 us
  Pallas kernels  42.3 us (93%)
  local copies, waits for them, and re-layouts  2.53 us (6%)
  between operations  0.65 us (1%)
    pallas_call x1, Pallas kernels, shards(): pl.pallas_call(kernel, out_shape=(jax.ShapeDtypeStruct(adjoint_in.shape,...  42.3 us
    unnamed x4, local copies, waits for them, and re-layouts  2.53 us

profile of v3, /device:TPU:5, one launch (start us, length us, event | category | flops | bytes accessed | tf_op | source)
XLA Modules:
  0.0 45.5 jit_solution(16447228891682512540)
XLA Ops:
  0.6 42.3 %shard_map.122 = (f32[9,8,16,128]{3,2,1,0:T(8,128)}, f32[3,16,128]{2,1,0:T(8,128)}) custom-call(f32[9,8,16,128]{3,2,1,0:T(8,128)} %adj_hbm.1, bf16[3,9,8,16,128]{4,3,2,1,0:T(8,128)(2,1)} %traj_hbm.1, f32[2,8,16,128]{3,2,1,0:T(8,128)} %cour_hbm.1, f32[8,16,128]{2,1,0:T(8,128)} %mix_hbm.1, s32[16,128]{1,0:T(8,128)} %land_hbm.1, s32[16,128]{1,0:T(8,128)} %srcm_hbm.1, ...), custom_call_target="tpu_custom_call" | custom-call | tf_op jit(solution)/shard_map/pallas_call | solution.py:388
  42.9 0.0 copy-start
  42.9 1.9 %copy.15 = f32[9,8,16,128]{3,2,1,0:T(8,128)} copy(f32[9,8,16,128]{3,2,1,0:T(8,128)} %get-tuple-element.4) | data formatting | bytes 1179648
  44.9 0.0 copy-done
  44.9 0.6 %copy.16 = f32[3,16,128]{2,1,0:T(8,128)} copy(f32[3,16,128]{2,1,0:T(8,128)S(1)} %copy-done) | data formatting | bytes 49152
Async XLA Ops:
  42.9 1.9 %copy-start = (f32[3,16,128]{2,1,0:T(8,128)S(1)}, f32[3,16,128]{2,1,0:T(8,128)}, u32[]{:S(2)}) copy-start(f32[3,16,128]{2,1,0:T(8,128)} %get-tuple-element.5) | copy-start | bytes 73732

commit v4 on v3

--- a/solution.py
+++ b/solution.py
@@ -18,7 +18,7 @@
     rates_hbm, speed_hbm, sclass_hbm, prof_hbm, ecoef_hbm,
     out_hbm, emis_hbm,
     out_ref, emis_ref, land_ref, srcm_ref, rates_ref, speed_ref, sclass_ref, prof_ref, ecoef_ref,
-    traj_ref, cour_ref, mix_ref, pad_ref, at_ref, ht_ref, hb_ref, lv_ref, eo_ref, ep_ref,
+    traj_ref, cour_ref, mix_ref, pad_ref, lh_ref, at_ref, ht_ref, hb_ref, lv_ref, eo_ref, ep_ref,
     cx_ref, cy_ref, vc_ref, cet_ref, ceh_ref, cyp_ref, mh_ref,
     send_sem, recv_sem, local_sem,
 ):
@@ -74,6 +74,7 @@
     for k in range(steps):
         pad_ref[k, :, :, 0:PAD, :] = zeros_pad
         pad_ref[k, :, :, PAD + n_y : 2 * PAD + n_y, :] = zeros_pad
+        lh_ref[k] = zeros_pad
     zeros_c = jnp.zeros((n_z, PAD, n_x), jnp.float32)
     cyp_ref[:, 0:PAD, :] = zeros_c
     cyp_ref[:, PAD + n_y : 2 * PAD + n_y, :] = zeros_c
@@ -273,13 +274,13 @@
 
         lat_up = rcopy(
             pad_ref.at[k, :, :, pl.ds(PAD + n_y - 2, 2), :],
-            pad_ref.at[k, :, :, pl.ds(PAD - 2, 2), :],
+            lh_ref.at[k, :, :, pl.ds(0, 2), :],
             S_UP + k,
             (lon, up, lev),
         )
         lat_down = rcopy(
             pad_ref.at[k, :, :, pl.ds(PAD, 2), :],
-            pad_ref.at[k, :, :, pl.ds(PAD + n_y, 2), :],
+            lh_ref.at[k, :, :, pl.ds(2, 2), :],
             S_DOWN + k,
             (lon, down, lev),
         )
@@ -307,35 +308,18 @@
         if k == steps - 1:
             build_transport_coefficients()
 
-        lon_right.wait()
-        lon_left.wait()
-
-        @pl.when(has_up)
-        def _():
-            lat_up.wait_send()
-            lat_down.wait_recv()
-
-        @pl.when(has_down)
-        def _():
-            lat_down.wait_send()
-            lat_up.wait_recv()
-
-        for t in range(n_t):
-            hb_ref[t] = ht_ref[k, :, t * rows : (t + 1) * rows].T.reshape(n_z, n_y, n_x)
-
         def transport(i, carry):
             t = i // n_z
             z = i % n_z
             a = pad_ref[k, t, z, PAD : PAD + n_y, :]
-            hz = hb_ref[t, z]
             y_p1 = pad_ref[k, t, z, PAD + 1 : PAD + 1 + n_y, :]
             y_p2 = pad_ref[k, t, z, PAD + 2 : PAD + 2 + n_y, :]
             y_m1 = pad_ref[k, t, z, PAD - 1 : PAD - 1 + n_y, :]
             y_m2 = pad_ref[k, t, z, PAD - 2 : PAD - 2 + n_y, :]
-            x_p1 = jnp.where(lane == n_x - 1, pltpu.roll(hz, n_x - 1, 1), pltpu.roll(a, n_x - 1, 1))
-            x_p2 = jnp.where(lane >= n_x - 2, pltpu.roll(hz, n_x - 2, 1), pltpu.roll(a, n_x - 2, 1))
-            x_m1 = jnp.where(lane == 0, pltpu.roll(hz, 1, 1), pltpu.roll(a, 1, 1))
-            x_m2 = jnp.where(lane <= 1, pltpu.roll(hz, 2, 1), pltpu.roll(a, 2, 1))
+            x_p1 = pltpu.roll(a, n_x - 1, 1)
+            x_p2 = pltpu.roll(a, n_x - 2, 1)
+            x_m1 = pltpu.roll(a, 1, 1)
+            x_m2 = pltpu.roll(a, 2, 1)
             lon_part = (
                 cx_ref[0, z] * (a - x_p1)
                 + cx_ref[1, z] * (x_p1 - x_p2)
@@ -352,6 +336,56 @@
             return carry
 
         lax.fori_loop(0, n_t * n_z, transport, 0, unroll=4)
+
+        lon_right.wait()
+        lon_left.wait()
+
+        @pl.when(has_up)
+        def _():
+            lat_up.wait_send()
+            lat_down.wait_recv()
+
+        @pl.when(has_down)
+        def _():
+            lat_down.wait_send()
+            lat_up.wait_recv()
+
+        for t in range(n_t):
+            hb_ref[t] = ht_ref[k, :, t * rows : (t + 1) * rows].T.reshape(n_z, n_y, n_x)
+
+        def edges(i, carry):
+            t = i // n_z
+            z = i % n_z
+            a = pad_ref[k, t, z, PAD : PAD + n_y, :]
+            d = hb_ref[t, z] - a
+            d_m1 = pltpu.roll(d, 1, 1)
+            d_m2 = pltpu.roll(d, 2, 1)
+            d_p1 = pltpu.roll(d, n_x - 1, 1)
+            d_p2 = pltpu.roll(d, n_x - 2, 1)
+            cx0 = cx_ref[0, z]
+            cx1 = cx_ref[1, z]
+            cxm1 = cx_ref[2, z]
+            cxm2 = cx_ref[3, z]
+            low = cxm2 * d_m2 + jnp.where(lane == 0, (cxm1 - cxm2) * d_m1, 0.0)
+            high = jnp.where(lane == n_x - 1, (cx1 - cx0) * d_p1, 0.0) - cx1 * d_p2
+            corr = jnp.where(lane <= 1, low, jnp.where(lane >= n_x - 2, high, 0.0))
+            out_ref[t, z] = out_ref[t, z] + corr
+            h = lh_ref[k, t, z, 0:4, :]
+            am2 = h[0:1]
+            am1 = h[1:2]
+            ap1 = h[2:3]
+            ap2 = h[3:4]
+            c_lo = cy_ref[:, z, 0:2, :]
+            c_hi = cy_ref[:, z, n_y - 2 : n_y, :]
+            r0 = c_lo[2, 0:1] * am1 + c_lo[3, 0:1] * (am2 - am1)
+            r1 = c_lo[3, 1:2] * am1
+            r14 = -c_hi[1, 0:1] * ap1
+            r15 = c_hi[1, 1:2] * (ap1 - ap2) - c_hi[0, 1:2] * ap1
+            out_ref[t, z, 0:2, :] = out_ref[t, z, 0:2, :] + jnp.concatenate([r0, r1], axis=0)
+            out_ref[t, z, n_y - 2 : n_y, :] = out_ref[t, z, n_y - 2 : n_y, :] + jnp.concatenate([r14, r15], axis=0)
+            return carry
+
+        lax.fori_loop(0, n_t * n_z, edges, 0, unroll=4)
 
     emis_copy = rcopy(eo_ref, ep_ref, S_EMIS, (lon, lat, partner))
     emis_copy.start()
@@ -407,6 +441,7 @@
             pltpu.VMEM(courant.shape, f32),
             pltpu.VMEM(mixing.shape, f32),
             pltpu.VMEM((steps, n_t, n_z, n_y + 2 * PAD, n_x), f32),
+            pltpu.VMEM((steps, n_t, n_z, PAD, n_x), f32),
             pltpu.VMEM((steps, n_x, n_t * rows), f32),
             pltpu.VMEM((steps, n_x, n_t * rows), f32),
             pltpu.VMEM((n_t, n_z, n_y, n_x), f32),

time: 45.6 us -> 44.3 us (0.971)
  Pallas kernels: 42.3 us -> 41 us
    pallas_call x1, Pallas kernels: 42.3 us -> 41 us  [shards(): pl.pallas_call(kernel, out_shape=(jax.ShapeDtypeStruct(adjoint_in.shape,...]
where the time goes in v4:
time: 44.3 us; the launch traced here: 44.2 us
  Pallas kernels  41 us (93%)
  local copies, waits for them, and re-layouts  2.53 us (6%)
  between operations  0.65 us (1%)
    pallas_call x1, Pallas kernels, shards(): pl.pallas_call(kernel, out_shape=(jax.ShapeDtypeStruct(adjoint_in.shape,...  41 us
    unnamed x4, local copies, waits for them, and re-layouts  2.53 us

profile of v4, /device:TPU:5, one launch (start us, length us, event | category | flops | bytes accessed | tf_op | source)
XLA Modules:
  0.0 44.2 jit_solution(17394403694453769370)
XLA Ops:
  0.6 41.0 %shard_map.122 = (f32[9,8,16,128]{3,2,1,0:T(8,128)}, f32[3,16,128]{2,1,0:T(8,128)}) custom-call(f32[9,8,16,128]{3,2,1,0:T(8,128)} %adj_hbm.1, bf16[3,9,8,16,128]{4,3,2,1,0:T(8,128)(2,1)} %traj_hbm.1, f32[2,8,16,128]{3,2,1,0:T(8,128)} %cour_hbm.1, f32[8,16,128]{2,1,0:T(8,128)} %mix_hbm.1, s32[16,128]{1,0:T(8,128)} %land_hbm.1, s32[16,128]{1,0:T(8,128)} %srcm_hbm.1, ...), custom_call_target="tpu_custom_call" | custom-call | tf_op jit(solution)/shard_map/pallas_call | solution.py:422
  41.6 0.0 copy-start
  41.6 1.9 %copy.15 = f32[9,8,16,128]{3,2,1,0:T(8,128)} copy(f32[9,8,16,128]{3,2,1,0:T(8,128)} %get-tuple-element.4) | data formatting | bytes 1179648
  43.6 0.0 copy-done
  43.6 0.6 %copy.16 = f32[3,16,128]{2,1,0:T(8,128)} copy(f32[3,16,128]{2,1,0:T(8,128)S(1)} %copy-done) | data formatting | bytes 49152
Async XLA Ops:
  41.6 1.9 %copy-start = (f32[3,16,128]{2,1,0:T(8,128)S(1)}, f32[3,16,128]{2,1,0:T(8,128)}, u32[]{:S(2)}) copy-start(f32[3,16,128]{2,1,0:T(8,128)} %get-tuple-element.5) | copy-start | bytes 73732

commit v5 on v4

--- a/solution.py
+++ b/solution.py
@@ -257,21 +257,6 @@
         lax.fori_loop(0, n_t * (n_z - 1), vert_inner, 0, unroll=7)
         lev_copy.wait()
 
-        def vert_edge(t, carry):
-            z = edge_z
-            s = speed_ref[sclass_ref[level0 + z], t]
-            a = out_ref[t, z]
-            other = out_ref[t, inner_z]
-            halo = lv_ref[k, t, 0]
-            a_below = jnp.where(low_half, other, halo)
-            a_above = jnp.where(low_half, halo, other)
-            pad_ref[k, t, z, PAD : PAD + n_y, :] = (
-                a * (vc_ref[2, z] - s) + a_below * (vc_ref[1, z] + s) + a_above * vc_ref[0, z]
-            )
-            return carry
-
-        lax.fori_loop(0, n_t, vert_edge, 0, unroll=3)
-
         lat_up = rcopy(
             pad_ref.at[k, :, :, pl.ds(PAD + n_y - 2, 2), :],
             lh_ref.at[k, :, :, pl.ds(0, 2), :],
@@ -284,26 +269,55 @@
             S_DOWN + k,
             (lon, down, lev),
         )
-
-        @pl.when(has_up)
-        def _():
-            lat_up.start()
-
-        @pl.when(has_down)
-        def _():
-            lat_down.start()
-
-        for t in range(n_t):
-            blk = pad_ref[k, t, :, PAD : PAD + n_y, :].reshape(rows, n_x)
-            at_ref[k, :, t * rows : (t + 1) * rows] = blk.T
         lon_right = rcopy(
             at_ref.at[k, pl.ds(n_x - 2, 2), :], ht_ref.at[k, pl.ds(n_x - 2, 2), :], S_RIGHT + k, (right, lat, lev)
         )
         lon_left = rcopy(
             at_ref.at[k, pl.ds(0, 2), :], ht_ref.at[k, pl.ds(0, 2), :], S_LEFT + k, (left, lat, lev)
         )
-        lon_right.start()
-        lon_left.start()
+
+        for t in range(n_t):
+            z = edge_z
+            s = speed_ref[sclass_ref[level0 + z], t]
+            a = out_ref[t, z]
+            other = out_ref[t, inner_z]
+            halo = lv_ref[k, t, 0]
+            a_below = jnp.where(low_half, other, halo)
+            a_above = jnp.where(low_half, halo, other)
+            pad_ref[k, t, z, PAD : PAD + n_y, :] = (
+                a * (vc_ref[2, z] - s) + a_below * (vc_ref[1, z] + s) + a_above * vc_ref[0, z]
+            )
+            up_t = rcopy(
+                pad_ref.at[k, t, :, pl.ds(PAD + n_y - 2, 2), :],
+                lh_ref.at[k, t, :, pl.ds(0, 2), :],
+                S_UP + k,
+                (lon, up, lev),
+            )
+            down_t = rcopy(
+                pad_ref.at[k, t, :, pl.ds(PAD, 2), :],
+                lh_ref.at[k, t, :, pl.ds(2, 2), :],
+                S_DOWN + k,
+                (lon, down, lev),
+            )
+
+            @pl.when(has_up)
+            def _():
+                up_t.start()
+
+            @pl.when(has_down)
+            def _():
+                down_t.start()
+
+            blk = pad_ref[k, t, :, PAD : PAD + n_y, :].reshape(rows, n_x)
+            cols = pl.ds(t * rows, rows)
+            at_ref[k, :, cols] = blk.T
+            rcopy(
+                at_ref.at[k, pl.ds(n_x - 2, 2), cols], ht_ref.at[k, pl.ds(n_x - 2, 2), cols], S_RIGHT + k,
+                (right, lat, lev),
+            ).start()
+            rcopy(
+                at_ref.at[k, pl.ds(0, 2), cols], ht_ref.at[k, pl.ds(0, 2), cols], S_LEFT + k, (left, lat, lev)
+            ).start()
 
         if k == steps - 1:
             build_transport_coefficients()

time: 44.3 us -> 44.5 us (level)
  no operation moved by 1% of the time
where the time goes in v5:
time: 44.5 us; the launch traced here: 44.4 us
  Pallas kernels  41.3 us (93%)
  local copies, waits for them, and re-layouts  2.53 us (6%)
  between operations  0.65 us (1%)
    pallas_call x1, Pallas kernels, shards(): pl.pallas_call(kernel, out_shape=(jax.ShapeDtypeStruct(adjoint_in.shape,...  41.3 us
    unnamed x4, local copies, waits for them, and re-layouts  2.53 us

profile of v5, /device:TPU:5, one launch (start us, length us, event | category | flops | bytes accessed | tf_op | source)
XLA Modules:
  0.0 44.4 jit_solution(13330701245177025196)
XLA Ops:
  0.6 41.3 %shard_map.122 = (f32[9,8,16,128]{3,2,1,0:T(8,128)}, f32[3,16,128]{2,1,0:T(8,128)}) custom-call(f32[9,8,16,128]{3,2,1,0:T(8,128)} %adj_hbm.1, bf16[3,9,8,16,128]{4,3,2,1,0:T(8,128)(2,1)} %traj_hbm.1, f32[2,8,16,128]{3,2,1,0:T(8,128)} %cour_hbm.1, f32[8,16,128]{2,1,0:T(8,128)} %mix_hbm.1, s32[16,128]{1,0:T(8,128)} %land_hbm.1, s32[16,128]{1,0:T(8,128)} %srcm_hbm.1, ...), custom_call_target="tpu_custom_call" | custom-call | tf_op jit(solution)/shard_map/pallas_call | solution.py:436
  41.9 0.0 copy-start
  41.9 1.9 %copy.15 = f32[9,8,16,128]{3,2,1,0:T(8,128)} copy(f32[9,8,16,128]{3,2,1,0:T(8,128)} %get-tuple-element.4) | data formatting | bytes 1179648
  43.8 0.0 copy-done
  43.8 0.6 %copy.16 = f32[3,16,128]{2,1,0:T(8,128)} copy(f32[3,16,128]{2,1,0:T(8,128)S(1)} %copy-done) | data formatting | bytes 49152
Async XLA Ops:
  41.9 1.9 %copy-start = (f32[3,16,128]{2,1,0:T(8,128)S(1)}, f32[3,16,128]{2,1,0:T(8,128)}, u32[]{:S(2)}) copy-start(f32[3,16,128]{2,1,0:T(8,128)} %get-tuple-element.5) | copy-start | bytes 73732

commit v6 on v5

--- a/solution.py
+++ b/solution.py
@@ -79,20 +79,6 @@
     cyp_ref[:, 0:PAD, :] = zeros_c
     cyp_ref[:, PAD + n_y : 2 * PAD + n_y, :] = zeros_c
 
-    barrier = pltpu.get_barrier_semaphore()
-    for dev in ((lon, lat, partner), (left, lat, lev), (right, lat, lev)):
-        pl.semaphore_signal(barrier, 1, device_id=dev, device_id_type=MESH)
-
-    @pl.when(has_up)
-    def _():
-        pl.semaphore_signal(barrier, 1, device_id=(lon, up, lev), device_id_type=MESH)
-
-    @pl.when(has_down)
-    def _():
-        pl.semaphore_signal(barrier, 1, device_id=(lon, down, lev), device_id_type=MESH)
-
-    pl.semaphore_wait(barrier, 3 + has_up.astype(jnp.int32) + has_down.astype(jnp.int32))
-
     def rcopy(src, dst, idx, dev):
         return pltpu.make_async_remote_copy(
             src, dst, send_sem.at[idx], recv_sem.at[idx], device_id=dev, device_id_type=MESH
@@ -118,22 +104,29 @@
         cyp_ref.at[:, pl.ds(PAD, 2), :], cyp_ref.at[:, pl.ds(PAD + n_y, 2), :], S_CN_D, (lon, down, lev)
     )
     mix_x = rcopy(mix_ref.at[pl.ds(edge_z, 1)], mh_ref, S_MIX, (lon, lat, partner))
-    mix_x.start()
-    ce_right.start()
-    ce_left.start()
-
-    @pl.when(has_up)
-    def _():
-        cn_up.start()
-
-    @pl.when(has_down)
-    def _():
-        cn_down.start()
+
+    def start_coefficient_halos():
+        mix_x.start()
+        ce_right.start()
+        ce_left.start()
+
+        @pl.when(has_up)
+        def _():
+            cn_up.start()
+
+        @pl.when(has_down)
+        def _():
+            cn_down.start()
+
+    def fix_vertical_coefficients():
+        mix_x.wait()
+        below = jnp.where(low_half, vc_ref[1, 0], mh_ref[0])
+        vc_ref[1, 0] = below
+        vc_ref[2, 0] = jnp.where(low_half, vc_ref[2, 0], 1.0 - vc_ref[0, 0] - below)
 
     def build_vertical_coefficients():
-        mix_x.wait()
         dep = jnp.where(low_half, 0.1 + 0.3 * land_ref[...].astype(jnp.float32), 0.0)
-        below = jnp.where(low_half, 0.0, mh_ref[0])
+        below = jnp.zeros((n_y, n_x), jnp.float32)
         for z in range(n_z):
             above = mix_ref[z]
             if z == n_z - 1:
@@ -179,8 +172,11 @@
     eo_ref[...] = jnp.zeros(eo_ref.shape, jnp.float32)
     src_mask = srcm_ref[...].astype(jnp.float32)
     adj_in.wait()
+    build_vertical_coefficients()
+    emis_copy = rcopy(eo_ref, ep_ref, S_EMIS, (lon, lat, partner))
 
     for k in range(steps - 1, -1, -1):
+        first = k == steps - 1
         traj_in[k].wait()
 
         def coag_level(zz, acc):
@@ -233,13 +229,13 @@
         zero = jnp.zeros((n_y, n_x), jnp.float32)
         acc = coag_level(0, (zero, zero, zero))
         lev_copy = rcopy(out_ref.at[:, pl.ds(edge_z, 1)], lv_ref.at[k], S_LEV + k, (lon, lat, partner))
-        lev_copy.start()
+        if not first:
+            lev_copy.start()
         acc = lax.fori_loop(1, n_z, coag_level, acc)
         for m in range(3):
             eo_ref[m] = eo_ref[m] + acc[m] * src_mask
-
-        if k == steps - 1:
-            build_vertical_coefficients()
+        if k == 0:
+            emis_copy.start()
 
         def vert_inner(i, carry):
             t = i // (n_z - 1)
@@ -255,6 +251,23 @@
             return carry
 
         lax.fori_loop(0, n_t * (n_z - 1), vert_inner, 0, unroll=7)
+        if first:
+            barrier = pltpu.get_barrier_semaphore()
+            for dev in ((lon, lat, partner), (left, lat, lev), (right, lat, lev)):
+                pl.semaphore_signal(barrier, 1, device_id=dev, device_id_type=MESH)
+
+            @pl.when(has_up)
+            def _():
+                pl.semaphore_signal(barrier, 1, device_id=(lon, up, lev), device_id_type=MESH)
+
+            @pl.when(has_down)
+            def _():
+                pl.semaphore_signal(barrier, 1, device_id=(lon, down, lev), device_id_type=MESH)
+
+            pl.semaphore_wait(barrier, 3 + has_up.astype(jnp.int32) + has_down.astype(jnp.int32))
+            start_coefficient_halos()
+            lev_copy.start()
+            fix_vertical_coefficients()
         lev_copy.wait()
 
         lat_up = rcopy(
@@ -401,8 +414,6 @@
 
         lax.fori_loop(0, n_t * n_z, edges, 0, unroll=4)
 
-    emis_copy = rcopy(eo_ref, ep_ref, S_EMIS, (lon, lat, partner))
-    emis_copy.start()
     emis_copy.wait()
     emis_ref[...] = eo_ref[...] + ep_ref[...]
     out_copy = pltpu.make_async_copy(out_ref, out_hbm, local_sem.at[0])

time: 44.5 us -> 44.7 us (level)
  no operation moved by 1% of the time
where the time goes in v6:
time: 44.7 us; the launch traced here: 44.5 us
  Pallas kernels  41.4 us (93%)
  local copies, waits for them, and re-layouts  2.53 us (6%)
  between operations  0.65 us (1%)
    pallas_call x1, Pallas kernels, shards(): pl.pallas_call(kernel, out_shape=(jax.ShapeDtypeStruct(adjoint_in.shape,...  41.4 us
    unnamed x4, local copies, waits for them, and re-layouts  2.53 us

profile of v6, /device:TPU:5, one launch (start us, length us, event | category | flops | bytes accessed | tf_op | source)
XLA Modules:
  0.0 44.5 jit_solution(2565131367791168465)
XLA Ops:
  0.6 41.4 %shard_map.122 = (f32[9,8,16,128]{3,2,1,0:T(8,128)}, f32[3,16,128]{2,1,0:T(8,128)}) custom-call(f32[9,8,16,128]{3,2,1,0:T(8,128)} %adj_hbm.1, bf16[3,9,8,16,128]{4,3,2,1,0:T(8,128)(2,1)} %traj_hbm.1, f32[2,8,16,128]{3,2,1,0:T(8,128)} %cour_hbm.1, f32[8,16,128]{2,1,0:T(8,128)} %mix_hbm.1, s32[16,128]{1,0:T(8,128)} %land_hbm.1, s32[16,128]{1,0:T(8,128)} %srcm_hbm.1, ...), custom_call_target="tpu_custom_call" | custom-call | tf_op jit(solution)/shard_map/pallas_call | solution.py:447
  42.0 0.0 copy-start
  42.0 1.9 %copy.15 = f32[9,8,16,128]{3,2,1,0:T(8,128)} copy(f32[9,8,16,128]{3,2,1,0:T(8,128)} %get-tuple-element.4) | data formatting | bytes 1179648
  43.9 0.0 copy-done
  43.9 0.6 %copy.16 = f32[3,16,128]{2,1,0:T(8,128)} copy(f32[3,16,128]{2,1,0:T(8,128)S(1)} %copy-done) | data formatting | bytes 49152
Async XLA Ops:
  42.0 1.9 %copy-start = (f32[3,16,128]{2,1,0:T(8,128)S(1)}, f32[3,16,128]{2,1,0:T(8,128)}, u32[]{:S(2)}) copy-start(f32[3,16,128]{2,1,0:T(8,128)} %get-tuple-element.5) | copy-start | bytes 73732

commit v7 on v6

--- a/solution.py
+++ b/solution.py
@@ -424,6 +424,24 @@
     emis_out.wait()
 
 
+def hand_over(adj_hbm, emis_hbm, adj_out, emis_out, adj_buf, emis_buf, sem):
+    ins = [
+        pltpu.make_async_copy(adj_hbm, adj_buf, sem.at[0]),
+        pltpu.make_async_copy(emis_hbm, emis_buf, sem.at[1]),
+    ]
+    for c in ins:
+        c.start()
+    outs = [
+        pltpu.make_async_copy(adj_buf, adj_out, sem.at[2]),
+        pltpu.make_async_copy(emis_buf, emis_out, sem.at[3]),
+    ]
+    for c, o in zip(ins, outs):
+        c.wait()
+        o.start()
+    for o in outs:
+        o.wait()
+
+
 def shards(
     adjoint_in,
     trajectory,
@@ -444,7 +462,7 @@
     vmem = pl.BlockSpec(memory_space=pltpu.VMEM)
     smem = pl.BlockSpec(memory_space=pltpu.SMEM)
     f32 = jnp.float32
-    return pl.pallas_call(
+    adj_out, emis_out = pl.pallas_call(
         kernel,
         out_shape=(
             jax.ShapeDtypeStruct(adjoint_in.shape, f32),
@@ -491,6 +509,20 @@
         adjoint_in, trajectory, courant, mixing, land_mask, source_mask,
         coag_rates, settle_speed, settle_class, emis_profile, emis_coef,
     )
+    return pl.pallas_call(
+        hand_over,
+        out_shape=(
+            jax.ShapeDtypeStruct(adj_out.shape, f32),
+            jax.ShapeDtypeStruct(emis_out.shape, f32),
+        ),
+        in_specs=[hbm, hbm],
+        out_specs=(hbm, hbm),
+        scratch_shapes=[
+            pltpu.VMEM(adj_out.shape, f32),
+            pltpu.VMEM(emis_out.shape, f32),
+            pltpu.SemaphoreType.DMA((4,)),
+        ],
+    )(adj_out, emis_out)
 
 
 def solution(mesh):

time: 44.7 us -> 44 us (0.984)
  local copies, waits for them, and re-layouts: 2.53 us -> 0 us
  Pallas kernels: 41.4 us -> 43.3 us
    unnamed x4 -> x0, local copies, waits for them, and re-layouts: 2.53 us -> none
    pallas_call x0 -> x1, Pallas kernels: none -> 1.92 us  [shards(): pl.pallas_call(hand_over, out_shape=(jax.ShapeDtypeStruct(adj_out.shape,...]
where the time goes in v7:
time: 44 us; the launch traced here: 43.9 us
  Pallas kernels  43.3 us (98%)
  between operations  0.64 us (1%)
    pallas_call x1, Pallas kernels, shards(): pl.pallas_call(kernel, out_shape=(jax.ShapeDtypeStruct(adjoint_in.shape,...  41.4 us
    pallas_call x1, Pallas kernels, shards(): pl.pallas_call(hand_over, out_shape=(jax.ShapeDtypeStruct(adj_out.shape,...  1.92 us

profile of v7, /device:TPU:5, one launch (start us, length us, event | category | flops | bytes accessed | tf_op | source)
XLA Modules:
  0.0 43.9 jit_solution(1202513004919508055)
XLA Ops:
  0.6 41.4 %shard_map.122 = (f32[9,8,16,128]{3,2,1,0:T(8,128)}, f32[3,16,128]{2,1,0:T(8,128)}) custom-call(f32[9,8,16,128]{3,2,1,0:T(8,128)} %adj_hbm.1, bf16[3,9,8,16,128]{4,3,2,1,0:T(8,128)(2,1)} %traj_hbm.1, f32[2,8,16,128]{3,2,1,0:T(8,128)} %cour_hbm.1, f32[8,16,128]{2,1,0:T(8,128)} %mix_hbm.1, s32[16,128]{1,0:T(8,128)} %land_hbm.1, s32[16,128]{1,0:T(8,128)} %srcm_hbm.1, ...), custom_call_target="tpu_custom_call" | custom-call | tf_op jit(solution)/shard_map/pallas_call | solution.py:465
  42.0 1.9 %shard_map.123 = (f32[9,8,16,128]{3,2,1,0:T(8,128)}, f32[3,16,128]{2,1,0:T(8,128)}) custom-call(f32[9,8,16,128]{3,2,1,0:T(8,128)} %get-tuple-element.4.adj_hbm, f32[3,16,128]{2,1,0:T(8,128)} %get-tuple-element.5.emis_hbm), custom_call_target="tpu_custom_call" | custom-call | tf_op jit(solution)/shard_map/pallas_call | solution.py:512

commit v8 on v7

--- a/solution.py
+++ b/solution.py
@@ -237,20 +237,19 @@
         if k == 0:
             emis_copy.start()
 
-        def vert_inner(i, carry):
-            t = i // (n_z - 1)
-            z = i % (n_z - 1) + lev
-            zg = level0 + z
-            s = speed_ref[sclass_ref[zg], t]
-            a = out_ref[t, z]
-            a_below = jnp.where(z > 0, out_ref[t, jnp.maximum(z - 1, 0)], 0.0)
-            a_above = jnp.where(z < n_z - 1, out_ref[t, jnp.minimum(z + 1, n_z - 1)], 0.0)
-            pad_ref[k, t, z, PAD : PAD + n_y, :] = (
-                a * (vc_ref[2, z] - s) + a_below * (vc_ref[1, z] + s) + a_above * vc_ref[0, z]
-            )
+        def vert_inner(t, carry):
+            col = [out_ref[t, z] for z in range(n_z)]
+            for z in range(n_z):
+                s = speed_ref[sclass_ref[level0 + z], t]
+                val = col[z] * (vc_ref[2, z] - s)
+                if z > 0:
+                    val = val + col[z - 1] * (vc_ref[1, z] + s)
+                if z < n_z - 1:
+                    val = val + col[z + 1] * vc_ref[0, z]
+                pad_ref[k, t, z, PAD : PAD + n_y, :] = val
             return carry
 
-        lax.fori_loop(0, n_t * (n_z - 1), vert_inner, 0, unroll=7)
+        lax.fori_loop(0, n_t, vert_inner, 0)
         if first:
             barrier = pltpu.get_barrier_semaphore()
             for dev in ((lon, lat, partner), (left, lat, lev), (right, lat, lev)):

time: 44 us -> 43.3 us (0.984)
  Pallas kernels: 43.3 us -> 42.5 us
    pallas_call x1, Pallas kernels: 41.4 us -> 40.6 us  [shards(): pl.pallas_call(kernel, out_shape=(jax.ShapeDtypeStruct(adjoint_in.shape,...]
where the time goes in v8:
time: 43.3 us; the launch traced here: 43.1 us
  Pallas kernels  42.5 us (98%)
  between operations  0.64 us (1%)
    pallas_call x1, Pallas kernels, shards(): pl.pallas_call(kernel, out_shape=(jax.ShapeDtypeStruct(adjoint_in.shape,...  40.6 us
    pallas_call x1, Pallas kernels, shards(): pl.pallas_call(hand_over, out_shape=(jax.ShapeDtypeStruct(adj_out.shape,...  1.92 us

profile of v8, /device:TPU:5, one launch (start us, length us, event | category | flops | bytes accessed | tf_op | source)
XLA Modules:
  0.0 43.1 jit_solution(16035410761142296018)
XLA Ops:
  0.6 40.6 %shard_map.122 = (f32[9,8,16,128]{3,2,1,0:T(8,128)}, f32[3,16,128]{2,1,0:T(8,128)}) custom-call(f32[9,8,16,128]{3,2,1,0:T(8,128)} %adj_hbm.1, bf16[3,9,8,16,128]{4,3,2,1,0:T(8,128)(2,1)} %traj_hbm.1, f32[2,8,16,128]{3,2,1,0:T(8,128)} %cour_hbm.1, f32[8,16,128]{2,1,0:T(8,128)} %mix_hbm.1, s32[16,128]{1,0:T(8,128)} %land_hbm.1, s32[16,128]{1,0:T(8,128)} %srcm_hbm.1, ...), custom_call_target="tpu_custom_call" | custom-call | tf_op jit(solution)/shard_map/pallas_call | solution.py:464
  41.2 1.9 %shard_map.123 = (f32[9,8,16,128]{3,2,1,0:T(8,128)}, f32[3,16,128]{2,1,0:T(8,128)}) custom-call(f32[9,8,16,128]{3,2,1,0:T(8,128)} %get-tuple-element.4.adj_hbm, f32[3,16,128]{2,1,0:T(8,128)} %get-tuple-element.5.emis_hbm), custom_call_target="tpu_custom_call" | custom-call | tf_op jit(solution)/shard_map/pallas_call | solution.py:511

commit v9 on v8

--- a/solution.py
+++ b/solution.py
@@ -366,20 +366,10 @@
         lon_right.wait()
         lon_left.wait()
 
-        @pl.when(has_up)
-        def _():
-            lat_up.wait_send()
-            lat_down.wait_recv()
-
-        @pl.when(has_down)
-        def _():
-            lat_down.wait_send()
-            lat_up.wait_recv()
-
         for t in range(n_t):
             hb_ref[t] = ht_ref[k, :, t * rows : (t + 1) * rows].T.reshape(n_z, n_y, n_x)
 
-        def edges(i, carry):
+        def lon_edges(i, carry):
             t = i // n_z
             z = i % n_z
             a = pad_ref[k, t, z, PAD : PAD + n_y, :]
@@ -396,6 +386,23 @@
             high = jnp.where(lane == n_x - 1, (cx1 - cx0) * d_p1, 0.0) - cx1 * d_p2
             corr = jnp.where(lane <= 1, low, jnp.where(lane >= n_x - 2, high, 0.0))
             out_ref[t, z] = out_ref[t, z] + corr
+            return carry
+
+        lax.fori_loop(0, n_t * n_z, lon_edges, 0, unroll=4)
+
+        @pl.when(has_up)
+        def _():
+            lat_up.wait_send()
+            lat_down.wait_recv()
+
+        @pl.when(has_down)
+        def _():
+            lat_down.wait_send()
+            lat_up.wait_recv()
+
+        def lat_edges(i, carry):
+            t = i // n_z
+            z = i % n_z
             h = lh_ref[k, t, z, 0:4, :]
             am2 = h[0:1]
             am1 = h[1:2]
@@ -411,7 +418,7 @@
             out_ref[t, z, n_y - 2 : n_y, :] = out_ref[t, z, n_y - 2 : n_y, :] + jnp.concatenate([r14, r15], axis=0)
             return carry
 
-        lax.fori_loop(0, n_t * n_z, edges, 0, unroll=4)
+        lax.fori_loop(0, n_t * n_z, lat_edges, 0, unroll=4)
 
     emis_copy.wait()
     emis_ref[...] = eo_ref[...] + ep_ref[...]

time: 43.3 us -> 42.5 us (0.982)
  the two profiles are of different devices: /device:TPU:5 before, /device:TPU:1 now
where the time goes in v9:
time: 42.5 us; the launch traced here: 42.4 us
  Pallas kernels  41.8 us (98%)
  between operations  0.64 us (2%)
    pallas_call x1, Pallas kernels, shards(): pl.pallas_call(kernel, out_shape=(jax.ShapeDtypeStruct(adjoint_in.shape,...  39.9 us
    pallas_call x1, Pallas kernels, shards(): pl.pallas_call(hand_over, out_shape=(jax.ShapeDtypeStruct(adj_out.shape,...  1.92 us

profile of v9, /device:TPU:1, one launch (start us, length us, event | category | flops | bytes accessed | tf_op | source)
XLA Modules:
  0.0 42.4 jit_solution(14255243684083506332)
XLA Ops:
  0.6 39.9 %shard_map.122 = (f32[9,8,16,128]{3,2,1,0:T(8,128)}, f32[3,16,128]{2,1,0:T(8,128)}) custom-call(f32[9,8,16,128]{3,2,1,0:T(8,128)} %adj_hbm.1, bf16[3,9,8,16,128]{4,3,2,1,0:T(8,128)(2,1)} %traj_hbm.1, f32[2,8,16,128]{3,2,1,0:T(8,128)} %cour_hbm.1, f32[8,16,128]{2,1,0:T(8,128)} %mix_hbm.1, s32[16,128]{1,0:T(8,128)} %land_hbm.1, s32[16,128]{1,0:T(8,128)} %srcm_hbm.1, ...), custom_call_target="tpu_custom_call" | custom-call | tf_op jit(solution)/shard_map/pallas_call | solution.py:471
  40.5 1.9 %shard_map.123 = (f32[9,8,16,128]{3,2,1,0:T(8,128)}, f32[3,16,128]{2,1,0:T(8,128)}) custom-call(f32[9,8,16,128]{3,2,1,0:T(8,128)} %get-tuple-element.4.adj_hbm, f32[3,16,128]{2,1,0:T(8,128)} %get-tuple-element.5.emis_hbm), custom_call_target="tpu_custom_call" | custom-call | tf_op jit(solution)/shard_map/pallas_call | solution.py:518

commit v10 on v9

--- a/solution.py
+++ b/solution.py
@@ -320,6 +320,7 @@
             def _():
                 down_t.start()
 
+        for t in range(n_t):
             blk = pad_ref[k, t, :, PAD : PAD + n_y, :].reshape(rows, n_x)
             cols = pl.ds(t * rows, rows)
             at_ref[k, :, cols] = blk.T

time: 42.5 us -> 42.2 us (level)
  no operation moved by 1% of the time
where the time goes in v10:
time: 42.2 us; the launch traced here: 42.1 us
  Pallas kernels  41.4 us (98%)
  between operations  0.64 us (2%)
    pallas_call x1, Pallas kernels, shards(): pl.pallas_call(kernel, out_shape=(jax.ShapeDtypeStruct(adjoint_in.shape,...  39.5 us
    pallas_call x1, Pallas kernels, shards(): pl.pallas_call(hand_over, out_shape=(jax.ShapeDtypeStruct(adj_out.shape,...  1.92 us

profile of v10, /device:TPU:1, one launch (start us, length us, event | category | flops | bytes accessed | tf_op | source)
XLA Modules:
  0.0 42.1 jit_solution(9486398647636912856)
XLA Ops:
  0.6 39.5 %shard_map.122 = (f32[9,8,16,128]{3,2,1,0:T(8,128)}, f32[3,16,128]{2,1,0:T(8,128)}) custom-call(f32[9,8,16,128]{3,2,1,0:T(8,128)} %adj_hbm.1, bf16[3,9,8,16,128]{4,3,2,1,0:T(8,128)(2,1)} %traj_hbm.1, f32[2,8,16,128]{3,2,1,0:T(8,128)} %cour_hbm.1, f32[8,16,128]{2,1,0:T(8,128)} %mix_hbm.1, s32[16,128]{1,0:T(8,128)} %land_hbm.1, s32[16,128]{1,0:T(8,128)} %srcm_hbm.1, ...), custom_call_target="tpu_custom_call" | custom-call | tf_op jit(solution)/shard_map/pallas_call | solution.py:472
  40.2 1.9 %shard_map.123 = (f32[9,8,16,128]{3,2,1,0:T(8,128)}, f32[3,16,128]{2,1,0:T(8,128)}) custom-call(f32[9,8,16,128]{3,2,1,0:T(8,128)} %get-tuple-element.4.adj_hbm, f32[3,16,128]{2,1,0:T(8,128)} %get-tuple-element.5.emis_hbm), custom_call_target="tpu_custom_call" | custom-call | tf_op jit(solution)/shard_map/pallas_call | solution.py:519

commit v11 on v10

--- a/solution.py
+++ b/solution.py
@@ -367,29 +367,27 @@
         lon_right.wait()
         lon_left.wait()
 
-        for t in range(n_t):
-            hb_ref[t] = ht_ref[k, :, t * rows : (t + 1) * rows].T.reshape(n_z, n_y, n_x)
-
-        def lon_edges(i, carry):
-            t = i // n_z
-            z = i % n_z
-            a = pad_ref[k, t, z, PAD : PAD + n_y, :]
-            d = hb_ref[t, z] - a
-            d_m1 = pltpu.roll(d, 1, 1)
-            d_m2 = pltpu.roll(d, 2, 1)
-            d_p1 = pltpu.roll(d, n_x - 1, 1)
-            d_p2 = pltpu.roll(d, n_x - 2, 1)
-            cx0 = cx_ref[0, z]
-            cx1 = cx_ref[1, z]
-            cxm1 = cx_ref[2, z]
-            cxm2 = cx_ref[3, z]
-            low = cxm2 * d_m2 + jnp.where(lane == 0, (cxm1 - cxm2) * d_m1, 0.0)
-            high = jnp.where(lane == n_x - 1, (cx1 - cx0) * d_p1, 0.0) - cx1 * d_p2
-            corr = jnp.where(lane <= 1, low, jnp.where(lane >= n_x - 2, high, 0.0))
-            out_ref[t, z] = out_ref[t, z] + corr
+        def lon_edges(t, carry):
+            cols = pl.ds(pl.multiple_of(t * rows, rows), rows)
+            h_t = ht_ref[k, :, cols].T.reshape(n_z, n_y, n_x)
+            for z in range(n_z):
+                a = pad_ref[k, t, z, PAD : PAD + n_y, :]
+                d = h_t[z] - a
+                d_m1 = pltpu.roll(d, 1, 1)
+                d_m2 = pltpu.roll(d, 2, 1)
+                d_p1 = pltpu.roll(d, n_x - 1, 1)
+                d_p2 = pltpu.roll(d, n_x - 2, 1)
+                cx0 = cx_ref[0, z]
+                cx1 = cx_ref[1, z]
+                cxm1 = cx_ref[2, z]
+                cxm2 = cx_ref[3, z]
+                low = cxm2 * d_m2 + jnp.where(lane == 0, (cxm1 - cxm2) * d_m1, 0.0)
+                high = jnp.where(lane == n_x - 1, (cx1 - cx0) * d_p1, 0.0) - cx1 * d_p2
+                corr = jnp.where(lane <= 1, low, jnp.where(lane >= n_x - 2, high, 0.0))
+                out_ref[t, z] = out_ref[t, z] + corr
             return carry
 
-        lax.fori_loop(0, n_t * n_z, lon_edges, 0, unroll=4)
+        lax.fori_loop(0, n_t, lon_edges, 0)
 
         @pl.when(has_up)
         def _():

time: 42.2 us -> 41.9 us (level)
  the two profiles are of different devices: /device:TPU:1 before, /device:TPU:5 now
where the time goes in v11:
time: 41.9 us; the launch traced here: 41.1 us
  Pallas kernels  40.4 us (96%)
  between operations  0.64 us (2%)
    pallas_call x1, Pallas kernels, shards(): pl.pallas_call(kernel, out_shape=(jax.ShapeDtypeStruct(adjoint_in.shape,...  38.5 us
    pallas_call x1, Pallas kernels, shards(): pl.pallas_call(hand_over, out_shape=(jax.ShapeDtypeStruct(adj_out.shape,...  1.92 us

profile of v11, /device:TPU:5, one launch (start us, length us, event | category | flops | bytes accessed | tf_op | source)
XLA Modules:
  0.0 41.1 jit_solution(4199018851205101108)
XLA Ops:
  0.6 38.5 %shard_map.122 = (f32[9,8,16,128]{3,2,1,0:T(8,128)}, f32[3,16,128]{2,1,0:T(8,128)}) custom-call(f32[9,8,16,128]{3,2,1,0:T(8,128)} %adj_hbm.1, bf16[3,9,8,16,128]{4,3,2,1,0:T(8,128)(2,1)} %traj_hbm.1, f32[2,8,16,128]{3,2,1,0:T(8,128)} %cour_hbm.1, f32[8,16,128]{2,1,0:T(8,128)} %mix_hbm.1, s32[16,128]{1,0:T(8,128)} %land_hbm.1, s32[16,128]{1,0:T(8,128)} %srcm_hbm.1, ...), custom_call_target="tpu_custom_call" | custom-call | tf_op jit(solution)/shard_map/pallas_call | solution.py:470
  39.2 1.9 %shard_map.123 = (f32[9,8,16,128]{3,2,1,0:T(8,128)}, f32[3,16,128]{2,1,0:T(8,128)}) custom-call(f32[9,8,16,128]{3,2,1,0:T(8,128)} %get-tuple-element.4.adj_hbm, f32[3,16,128]{2,1,0:T(8,128)} %get-tuple-element.5.emis_hbm), custom_call_target="tpu_custom_call" | custom-call | tf_op jit(solution)/shard_map/pallas_call | solution.py:517

commit v12 on v11

--- a/solution.py
+++ b/solution.py
@@ -399,25 +399,24 @@
             lat_down.wait_send()
             lat_up.wait_recv()
 
-        def lat_edges(i, carry):
-            t = i // n_z
-            z = i % n_z
-            h = lh_ref[k, t, z, 0:4, :]
-            am2 = h[0:1]
-            am1 = h[1:2]
-            ap1 = h[2:3]
-            ap2 = h[3:4]
-            c_lo = cy_ref[:, z, 0:2, :]
-            c_hi = cy_ref[:, z, n_y - 2 : n_y, :]
-            r0 = c_lo[2, 0:1] * am1 + c_lo[3, 0:1] * (am2 - am1)
-            r1 = c_lo[3, 1:2] * am1
-            r14 = -c_hi[1, 0:1] * ap1
-            r15 = c_hi[1, 1:2] * (ap1 - ap2) - c_hi[0, 1:2] * ap1
-            out_ref[t, z, 0:2, :] = out_ref[t, z, 0:2, :] + jnp.concatenate([r0, r1], axis=0)
-            out_ref[t, z, n_y - 2 : n_y, :] = out_ref[t, z, n_y - 2 : n_y, :] + jnp.concatenate([r14, r15], axis=0)
+        def lat_edges(t, carry):
+            for z in range(n_z):
+                h = lh_ref[k, t, z, 0:4, :]
+                am2 = h[0:1]
+                am1 = h[1:2]
+                ap1 = h[2:3]
+                ap2 = h[3:4]
+                c_lo = cy_ref[:, z, 0:2, :]
+                c_hi = cy_ref[:, z, n_y - 2 : n_y, :]
+                r0 = c_lo[2, 0:1] * am1 + c_lo[3, 0:1] * (am2 - am1)
+                r1 = c_lo[3, 1:2] * am1
+                r14 = -c_hi[1, 0:1] * ap1
+                r15 = c_hi[1, 1:2] * (ap1 - ap2) - c_hi[0, 1:2] * ap1
+                out_ref[t, z, 0:2, :] = out_ref[t, z, 0:2, :] + jnp.concatenate([r0, r1], axis=0)
+                out_ref[t, z, n_y - 2 : n_y, :] = out_ref[t, z, n_y - 2 : n_y, :] + jnp.concatenate([r14, r15], axis=0)
             return carry
 
-        lax.fori_loop(0, n_t * n_z, lat_edges, 0, unroll=4)
+        lax.fori_loop(0, n_t, lat_edges, 0)
 
     emis_copy.wait()
     emis_ref[...] = eo_ref[...] + ep_ref[...]

time: 41.9 us -> 40.6 us (0.969)
  the two profiles are of different devices: /device:TPU:5 before, /device:TPU:1 now
where the time goes in v12:
time: 40.6 us; the launch traced here: 40.5 us
  Pallas kernels  39.8 us (98%)
  between operations  0.64 us (2%)
    pallas_call x1, Pallas kernels, shards(): pl.pallas_call(kernel, out_shape=(jax.ShapeDtypeStruct(adjoint_in.shape,...  37.9 us
    pallas_call x1, Pallas kernels, shards(): pl.pallas_call(hand_over, out_shape=(jax.ShapeDtypeStruct(adj_out.shape,...  1.92 us

profile of v12, /device:TPU:1, one launch (start us, length us, event | category | flops | bytes accessed | tf_op | source)
XLA Modules:
  0.0 40.5 jit_solution(13227218234978572671)
XLA Ops:
  0.6 37.9 %shard_map.122 = (f32[9,8,16,128]{3,2,1,0:T(8,128)}, f32[3,16,128]{2,1,0:T(8,128)}) custom-call(f32[9,8,16,128]{3,2,1,0:T(8,128)} %adj_hbm.1, bf16[3,9,8,16,128]{4,3,2,1,0:T(8,128)(2,1)} %traj_hbm.1, f32[2,8,16,128]{3,2,1,0:T(8,128)} %cour_hbm.1, f32[8,16,128]{2,1,0:T(8,128)} %mix_hbm.1, s32[16,128]{1,0:T(8,128)} %land_hbm.1, s32[16,128]{1,0:T(8,128)} %srcm_hbm.1, ...), custom_call_target="tpu_custom_call" | custom-call | tf_op jit(solution)/shard_map/pallas_call | solution.py:469
  38.6 1.9 %shard_map.123 = (f32[9,8,16,128]{3,2,1,0:T(8,128)}, f32[3,16,128]{2,1,0:T(8,128)}) custom-call(f32[9,8,16,128]{3,2,1,0:T(8,128)} %get-tuple-element.4.adj_hbm, f32[3,16,128]{2,1,0:T(8,128)} %get-tuple-element.5.emis_hbm), custom_call_target="tpu_custom_call" | custom-call | tf_op jit(solution)/shard_map/pallas_call | solution.py:516

commit v13 on v12

--- a/solution.py
+++ b/solution.py
@@ -335,34 +335,33 @@
         if k == steps - 1:
             build_transport_coefficients()
 
-        def transport(i, carry):
-            t = i // n_z
-            z = i % n_z
-            a = pad_ref[k, t, z, PAD : PAD + n_y, :]
-            y_p1 = pad_ref[k, t, z, PAD + 1 : PAD + 1 + n_y, :]
-            y_p2 = pad_ref[k, t, z, PAD + 2 : PAD + 2 + n_y, :]
-            y_m1 = pad_ref[k, t, z, PAD - 1 : PAD - 1 + n_y, :]
-            y_m2 = pad_ref[k, t, z, PAD - 2 : PAD - 2 + n_y, :]
-            x_p1 = pltpu.roll(a, n_x - 1, 1)
-            x_p2 = pltpu.roll(a, n_x - 2, 1)
-            x_m1 = pltpu.roll(a, 1, 1)
-            x_m2 = pltpu.roll(a, 2, 1)
-            lon_part = (
-                cx_ref[0, z] * (a - x_p1)
-                + cx_ref[1, z] * (x_p1 - x_p2)
-                + cx_ref[2, z] * (x_m1 - a)
-                + cx_ref[3, z] * (x_m2 - x_m1)
-            )
-            lat_part = (
-                cy_ref[0, z] * (a - y_p1)
-                + cy_ref[1, z] * (y_p1 - y_p2)
-                + cy_ref[2, z] * (y_m1 - a)
-                + cy_ref[3, z] * (y_m2 - y_m1)
-            )
-            out_ref[t, z] = a + lon_part + lat_part
+        def transport(t, carry):
+            for z in range(n_z):
+                a = pad_ref[k, t, z, PAD : PAD + n_y, :]
+                y_p1 = pad_ref[k, t, z, PAD + 1 : PAD + 1 + n_y, :]
+                y_p2 = pad_ref[k, t, z, PAD + 2 : PAD + 2 + n_y, :]
+                y_m1 = pad_ref[k, t, z, PAD - 1 : PAD - 1 + n_y, :]
+                y_m2 = pad_ref[k, t, z, PAD - 2 : PAD - 2 + n_y, :]
+                x_p1 = pltpu.roll(a, n_x - 1, 1)
+                x_p2 = pltpu.roll(a, n_x - 2, 1)
+                x_m1 = pltpu.roll(a, 1, 1)
+                x_m2 = pltpu.roll(a, 2, 1)
+                lon_part = (
+                    cx_ref[0, z] * (a - x_p1)
+                    + cx_ref[1, z] * (x_p1 - x_p2)
+                    + cx_ref[2, z] * (x_m1 - a)
+                    + cx_ref[3, z] * (x_m2 - x_m1)
+                )
+                lat_part = (
+                    cy_ref[0, z] * (a - y_p1)
+                    + cy_ref[1, z] * (y_p1 - y_p2)
+                    + cy_ref[2, z] * (y_m1 - a)
+                    + cy_ref[3, z] * (y_m2 - y_m1)
+                )
+                out_ref[t, z] = a + lon_part + lat_part
             return carry
 
-        lax.fori_loop(0, n_t * n_z, transport, 0, unroll=4)
+        lax.fori_loop(0, n_t, transport, 0)
 
         lon_right.wait()
         lon_left.wait()

time: 40.6 us -> 40.2 us (level)
  the two profiles are of different devices: /device:TPU:1 before, /device:TPU:5 now
where the time goes in v13:
time: 40.2 us; the launch traced here: 39.5 us
  Pallas kernels  38.8 us (97%)
  between operations  0.64 us (2%)
    pallas_call x1, Pallas kernels, shards(): pl.pallas_call(kernel, out_shape=(jax.ShapeDtypeStruct(adjoint_in.shape,...  36.9 us
    pallas_call x1, Pallas kernels, shards(): pl.pallas_call(hand_over, out_shape=(jax.ShapeDtypeStruct(adj_out.shape,...  1.92 us

profile of v13, /device:TPU:5, one launch (start us, length us, event | category | flops | bytes accessed | tf_op | source)
XLA Modules:
  0.0 39.5 jit_solution(10888887289510676579)
XLA Ops:
  0.6 36.9 %shard_map.122 = (f32[9,8,16,128]{3,2,1,0:T(8,128)}, f32[3,16,128]{2,1,0:T(8,128)}) custom-call(f32[9,8,16,128]{3,2,1,0:T(8,128)} %adj_hbm.1, bf16[3,9,8,16,128]{4,3,2,1,0:T(8,128)(2,1)} %traj_hbm.1, f32[2,8,16,128]{3,2,1,0:T(8,128)} %cour_hbm.1, f32[8,16,128]{2,1,0:T(8,128)} %mix_hbm.1, s32[16,128]{1,0:T(8,128)} %land_hbm.1, s32[16,128]{1,0:T(8,128)} %srcm_hbm.1, ...), custom_call_target="tpu_custom_call" | custom-call | tf_op jit(solution)/shard_map/pallas_call | solution.py:468
  37.6 1.9 %shard_map.123 = (f32[9,8,16,128]{3,2,1,0:T(8,128)}, f32[3,16,128]{2,1,0:T(8,128)}) custom-call(f32[9,8,16,128]{3,2,1,0:T(8,128)} %get-tuple-element.4.adj_hbm, f32[3,16,128]{2,1,0:T(8,128)} %get-tuple-element.5.emis_hbm), custom_call_target="tpu_custom_call" | custom-call | tf_op jit(solution)/shard_map/pallas_call | solution.py:515

commit v14 on v13

--- a/solution.py
+++ b/solution.py
@@ -231,7 +231,7 @@
         lev_copy = rcopy(out_ref.at[:, pl.ds(edge_z, 1)], lv_ref.at[k], S_LEV + k, (lon, lat, partner))
         if not first:
             lev_copy.start()
-        acc = lax.fori_loop(1, n_z, coag_level, acc)
+        acc = lax.fori_loop(1, n_z, coag_level, acc, unroll=True)
         for m in range(3):
             eo_ref[m] = eo_ref[m] + acc[m] * src_mask
         if k == 0:

time: 40.2 us -> 40.1 us (level)
  no operation moved by 1% of the time
where the time goes in v14:
time: 40.1 us; the launch traced here: 39.4 us
  Pallas kernels  38.8 us (97%)
  between operations  0.64 us (2%)
    pallas_call x1, Pallas kernels, shards(): pl.pallas_call(kernel, out_shape=(jax.ShapeDtypeStruct(adjoint_in.shape,...  36.9 us
    pallas_call x1, Pallas kernels, shards(): pl.pallas_call(hand_over, out_shape=(jax.ShapeDtypeStruct(adj_out.shape,...  1.92 us

profile of v14, /device:TPU:5, one launch (start us, length us, event | category | flops | bytes accessed | tf_op | source)
XLA Modules:
  0.0 39.4 jit_solution(4520520931311180095)
XLA Ops:
  0.6 36.9 %shard_map.122 = (f32[9,8,16,128]{3,2,1,0:T(8,128)}, f32[3,16,128]{2,1,0:T(8,128)}) custom-call(f32[9,8,16,128]{3,2,1,0:T(8,128)} %adj_hbm.1, bf16[3,9,8,16,128]{4,3,2,1,0:T(8,128)(2,1)} %traj_hbm.1, f32[2,8,16,128]{3,2,1,0:T(8,128)} %cour_hbm.1, f32[8,16,128]{2,1,0:T(8,128)} %mix_hbm.1, s32[16,128]{1,0:T(8,128)} %land_hbm.1, s32[16,128]{1,0:T(8,128)} %srcm_hbm.1, ...), custom_call_target="tpu_custom_call" | custom-call | tf_op jit(solution)/shard_map/pallas_call | solution.py:468
  37.5 1.9 %shard_map.123 = (f32[9,8,16,128]{3,2,1,0:T(8,128)}, f32[3,16,128]{2,1,0:T(8,128)}) custom-call(f32[9,8,16,128]{3,2,1,0:T(8,128)} %get-tuple-element.4.adj_hbm, f32[3,16,128]{2,1,0:T(8,128)} %get-tuple-element.5.emis_hbm), custom_call_target="tpu_custom_call" | custom-call | tf_op jit(solution)/shard_map/pallas_call | solution.py:515

commit v15 on v13

--- a/solution.py
+++ b/solution.py
@@ -19,7 +19,7 @@
     out_hbm, emis_hbm,
     out_ref, emis_ref, land_ref, srcm_ref, rates_ref, speed_ref, sclass_ref, prof_ref, ecoef_ref,
     traj_ref, cour_ref, mix_ref, pad_ref, lh_ref, at_ref, ht_ref, hb_ref, lv_ref, eo_ref, ep_ref,
-    cx_ref, cy_ref, vc_ref, cet_ref, ceh_ref, cyp_ref, mh_ref,
+    cx_ref, cy_ref, vc_ref, cet_ref, ceh_ref, cyp_ref, mh_ref, tw_ref,
     send_sem, recv_sem, local_sem,
 ):
     n_t, n_z, n_y, n_x = out_ref.shape
@@ -168,6 +168,17 @@
             cy_ref[1, z] = 0.5 * jnp.maximum(cyp_ref[z, PAD + 1 : PAD + 1 + n_y, :], 0.0)
             cy_ref[2, z] = -1.5 * jnp.minimum(cyp_ref[z, PAD - 1 : PAD - 1 + n_y, :], 0.0)
             cy_ref[3, z] = 0.5 * jnp.minimum(cyp_ref[z, PAD - 2 : PAD - 2 + n_y, :], 0.0)
+            x0, x1, xm1, xm2 = (cx_ref[i, z] for i in range(4))
+            y0, y1, ym1, ym2 = (cy_ref[i, z] for i in range(4))
+            tw_ref[0, z] = 1.0 + (x0 - xm1) + (y0 - ym1)
+            tw_ref[1, z] = x1 - x0
+            tw_ref[2, z] = -x1
+            tw_ref[3, z] = xm1 - xm2
+            tw_ref[4, z] = xm2
+            tw_ref[5, z] = y1 - y0
+            tw_ref[6, z] = -y1
+            tw_ref[7, z] = ym1 - ym2
+            tw_ref[8, z] = ym2
 
     eo_ref[...] = jnp.zeros(eo_ref.shape, jnp.float32)
     src_mask = srcm_ref[...].astype(jnp.float32)
@@ -346,19 +357,12 @@
                 x_p2 = pltpu.roll(a, n_x - 2, 1)
                 x_m1 = pltpu.roll(a, 1, 1)
                 x_m2 = pltpu.roll(a, 2, 1)
-                lon_part = (
-                    cx_ref[0, z] * (a - x_p1)
-                    + cx_ref[1, z] * (x_p1 - x_p2)
-                    + cx_ref[2, z] * (x_m1 - a)
-                    + cx_ref[3, z] * (x_m2 - x_m1)
+                out_ref[t, z] = (
+                    (tw_ref[0, z] * a + tw_ref[1, z] * x_p1 + tw_ref[2, z] * x_p2)
+                    + (tw_ref[3, z] * x_m1 + tw_ref[4, z] * x_m2)
+                    + (tw_ref[5, z] * y_p1 + tw_ref[6, z] * y_p2)
+                    + (tw_ref[7, z] * y_m1 + tw_ref[8, z] * y_m2)
                 )
-                lat_part = (
-                    cy_ref[0, z] * (a - y_p1)
-                    + cy_ref[1, z] * (y_p1 - y_p2)
-                    + cy_ref[2, z] * (y_m1 - a)
-                    + cy_ref[3, z] * (y_m2 - y_m1)
-                )
-                out_ref[t, z] = a + lon_part + lat_part
             return carry
 
         lax.fori_loop(0, n_t, transport, 0)
@@ -501,6 +505,7 @@
             pltpu.VMEM((n_x, rows), f32),
             pltpu.VMEM((n_z, n_y + 2 * PAD, n_x), f32),
             pltpu.VMEM((1, n_y, n_x), f32),
+            pltpu.VMEM((9, n_z, n_y, n_x), f32),
             pltpu.SemaphoreType.DMA((N_REMOTE,)),
             pltpu.SemaphoreType.DMA((N_REMOTE,)),
             pltpu.SemaphoreType.DMA((10 + steps,)),

time: 40.2 us -> 40.2 us (level)
  no operation moved by 1% of the time
where the time goes in v15:
time: 40.2 us; the launch traced here: 39.4 us
  Pallas kernels  38.8 us (97%)
  between operations  0.64 us (2%)
    pallas_call x1, Pallas kernels, shards(): pl.pallas_call(kernel, out_shape=(jax.ShapeDtypeStruct(adjoint_in.shape,...  36.9 us
    pallas_call x1, Pallas kernels, shards(): pl.pallas_call(hand_over, out_shape=(jax.ShapeDtypeStruct(adj_out.shape,...  1.92 us

profile of v15, /device:TPU:5, one launch (start us, length us, event | category | flops | bytes accessed | tf_op | source)
XLA Modules:
  0.0 39.4 jit_solution(9447099677393835192)
XLA Ops:
  0.6 36.9 %shard_map.122 = (f32[9,8,16,128]{3,2,1,0:T(8,128)}, f32[3,16,128]{2,1,0:T(8,128)}) custom-call(f32[9,8,16,128]{3,2,1,0:T(8,128)} %adj_hbm.1, bf16[3,9,8,16,128]{4,3,2,1,0:T(8,128)(2,1)} %traj_hbm.1, f32[2,8,16,128]{3,2,1,0:T(8,128)} %cour_hbm.1, f32[8,16,128]{2,1,0:T(8,128)} %mix_hbm.1, s32[16,128]{1,0:T(8,128)} %land_hbm.1, s32[16,128]{1,0:T(8,128)} %srcm_hbm.1, ...), custom_call_target="tpu_custom_call" | custom-call | tf_op jit(solution)/shard_map/pallas_call | solution.py:472
  37.5 1.9 %shard_map.123 = (f32[9,8,16,128]{3,2,1,0:T(8,128)}, f32[3,16,128]{2,1,0:T(8,128)}) custom-call(f32[9,8,16,128]{3,2,1,0:T(8,128)} %get-tuple-element.4.adj_hbm, f32[3,16,128]{2,1,0:T(8,128)} %get-tuple-element.5.emis_hbm), custom_call_target="tpu_custom_call" | custom-call | tf_op jit(solution)/shard_map/pallas_call | solution.py:520

commit v16 on v13

--- a/solution.py
+++ b/solution.py
@@ -175,6 +175,21 @@
     build_vertical_coefficients()
     emis_copy = rcopy(eo_ref, ep_ref, S_EMIS, (lon, lat, partner))
 
+    def lat_fix(k, t, z):
+        h = lh_ref[k, t, z, 0:4, :]
+        am2 = h[0:1]
+        am1 = h[1:2]
+        ap1 = h[2:3]
+        ap2 = h[3:4]
+        c_lo = cy_ref[:, z, 0:2, :]
+        c_hi = cy_ref[:, z, n_y - 2 : n_y, :]
+        r0 = c_lo[2, 0:1] * am1 + c_lo[3, 0:1] * (am2 - am1)
+        r1 = c_lo[3, 1:2] * am1
+        r14 = -c_hi[1, 0:1] * ap1
+        r15 = c_hi[1, 1:2] * (ap1 - ap2) - c_hi[0, 1:2] * ap1
+        out_ref[t, z, 0:2, :] = out_ref[t, z, 0:2, :] + jnp.concatenate([r0, r1], axis=0)
+        out_ref[t, z, n_y - 2 : n_y, :] = out_ref[t, z, n_y - 2 : n_y, :] + jnp.concatenate([r14, r15], axis=0)
+
     for k in range(steps - 1, -1, -1):
         first = k == steps - 1
         traj_in[k].wait()
@@ -182,6 +197,9 @@
         def coag_level(zz, acc):
             z = jnp.where(low_half, n_z - 1 - zz, zz)
             zg = level0 + z
+            if not first:
+                for t in range(n_t):
+                    lat_fix(k + 1, t, z)
             lam = [out_ref[t, z] for t in range(n_t)]
             st = [traj_ref[k, t, z].astype(jnp.float32) for t in range(n_t)]
             new_acc = []
@@ -398,24 +416,13 @@
             lat_down.wait_send()
             lat_up.wait_recv()
 
-        def lat_edges(t, carry):
-            for z in range(n_z):
-                h = lh_ref[k, t, z, 0:4, :]
-                am2 = h[0:1]
-                am1 = h[1:2]
-                ap1 = h[2:3]
-                ap2 = h[3:4]
-                c_lo = cy_ref[:, z, 0:2, :]
-                c_hi = cy_ref[:, z, n_y - 2 : n_y, :]
-                r0 = c_lo[2, 0:1] * am1 + c_lo[3, 0:1] * (am2 - am1)
-                r1 = c_lo[3, 1:2] * am1
-                r14 = -c_hi[1, 0:1] * ap1
-                r15 = c_hi[1, 1:2] * (ap1 - ap2) - c_hi[0, 1:2] * ap1
-                out_ref[t, z, 0:2, :] = out_ref[t, z, 0:2, :] + jnp.concatenate([r0, r1], axis=0)
-                out_ref[t, z, n_y - 2 : n_y, :] = out_ref[t, z, n_y - 2 : n_y, :] + jnp.concatenate([r14, r15], axis=0)
-            return carry
-
-        lax.fori_loop(0, n_t, lat_edges, 0)
+        if k == 0:
+            def lat_edges(t, carry):
+                for z in range(n_z):
+                    lat_fix(k, t, z)
+                return carry
+
+            lax.fori_loop(0, n_t, lat_edges, 0)
 
     emis_copy.wait()
     emis_ref[...] = eo_ref[...] + ep_ref[...]

time: 40.2 us -> 39.8 us (0.990)
    pallas_call x1, Pallas kernels: 36.9 us -> 36.5 us  [shards(): pl.pallas_call(kernel, out_shape=(jax.ShapeDtypeStruct(adjoint_in.shape,...]
where the time goes in v16:
time: 39.8 us; the launch traced here: 39.1 us
  Pallas kernels  38.4 us (96%)
  between operations  0.64 us (2%)
    pallas_call x1, Pallas kernels, shards(): pl.pallas_call(kernel, out_shape=(jax.ShapeDtypeStruct(adjoint_in.shape,...  36.5 us
    pallas_call x1, Pallas kernels, shards(): pl.pallas_call(hand_over, out_shape=(jax.ShapeDtypeStruct(adj_out.shape,...  1.92 us

profile of v16, /device:TPU:5, one launch (start us, length us, event | category | flops | bytes accessed | tf_op | source)
XLA Modules:
  0.0 39.1 jit_solution(14078790231193435521)
XLA Ops:
  0.6 36.5 %shard_map.122 = (f32[9,8,16,128]{3,2,1,0:T(8,128)}, f32[3,16,128]{2,1,0:T(8,128)}) custom-call(f32[9,8,16,128]{3,2,1,0:T(8,128)} %adj_hbm.1, bf16[3,9,8,16,128]{4,3,2,1,0:T(8,128)(2,1)} %traj_hbm.1, f32[2,8,16,128]{3,2,1,0:T(8,128)} %cour_hbm.1, f32[8,16,128]{2,1,0:T(8,128)} %mix_hbm.1, s32[16,128]{1,0:T(8,128)} %land_hbm.1, s32[16,128]{1,0:T(8,128)} %srcm_hbm.1, ...), custom_call_target="tpu_custom_call" | custom-call | tf_op jit(solution)/shard_map/pallas_call | solution.py:475
  37.2 1.9 %shard_map.123 = (f32[9,8,16,128]{3,2,1,0:T(8,128)}, f32[3,16,128]{2,1,0:T(8,128)}) custom-call(f32[9,8,16,128]{3,2,1,0:T(8,128)} %get-tuple-element.4.adj_hbm, f32[3,16,128]{2,1,0:T(8,128)} %get-tuple-element.5.emis_hbm), custom_call_target="tpu_custom_call" | custom-call | tf_op jit(solution)/shard_map/pallas_call | solution.py:522

commit v17 on v16

--- a/solution.py
+++ b/solution.py
@@ -420,6 +420,7 @@
             def lat_edges(t, carry):
                 for z in range(n_z):
                     lat_fix(k, t, z)
+                pltpu.make_async_copy(out_ref.at[t], out_hbm.at[t], local_sem.at[0]).start()
                 return carry
 
             lax.fori_loop(0, n_t, lat_edges, 0)
@@ -428,7 +429,6 @@
     emis_ref[...] = eo_ref[...] + ep_ref[...]
     out_copy = pltpu.make_async_copy(out_ref, out_hbm, local_sem.at[0])
     emis_out = pltpu.make_async_copy(emis_ref, emis_hbm, local_sem.at[1])
-    out_copy.start()
     emis_out.start()
     out_copy.wait()
     emis_out.wait()

time: 39.8 us -> 39.6 us (level)
  no operation moved by 1% of the time
where the time goes in v17:
time: 39.6 us; the launch traced here: 38.9 us
  Pallas kernels  38.3 us (97%)
  between operations  0.64 us (2%)
    pallas_call x1, Pallas kernels, shards(): pl.pallas_call(kernel, out_shape=(jax.ShapeDtypeStruct(adjoint_in.shape,...  36.3 us
    pallas_call x1, Pallas kernels, shards(): pl.pallas_call(hand_over, out_shape=(jax.ShapeDtypeStruct(adj_out.shape,...  1.92 us

profile of v17, /device:TPU:5, one launch (start us, length us, event | category | flops | bytes accessed | tf_op | source)
XLA Modules:
  0.0 38.9 jit_solution(2435617569341894365)
XLA Ops:
  0.6 36.3 %shard_map.122 = (f32[9,8,16,128]{3,2,1,0:T(8,128)}, f32[3,16,128]{2,1,0:T(8,128)}) custom-call(f32[9,8,16,128]{3,2,1,0:T(8,128)} %adj_hbm.1, bf16[3,9,8,16,128]{4,3,2,1,0:T(8,128)(2,1)} %traj_hbm.1, f32[2,8,16,128]{3,2,1,0:T(8,128)} %cour_hbm.1, f32[8,16,128]{2,1,0:T(8,128)} %mix_hbm.1, s32[16,128]{1,0:T(8,128)} %land_hbm.1, s32[16,128]{1,0:T(8,128)} %srcm_hbm.1, ...), custom_call_target="tpu_custom_call" | custom-call | tf_op jit(solution)/shard_map/pallas_call | solution.py:475
  37.0 1.9 %shard_map.123 = (f32[9,8,16,128]{3,2,1,0:T(8,128)}, f32[3,16,128]{2,1,0:T(8,128)}) custom-call(f32[9,8,16,128]{3,2,1,0:T(8,128)} %get-tuple-element.4.adj_hbm, f32[3,16,128]{2,1,0:T(8,128)} %get-tuple-element.5.emis_hbm), custom_call_target="tpu_custom_call" | custom-call | tf_op jit(solution)/shard_map/pallas_call | solution.py:522

commit v18 on v16

--- a/solution.py
+++ b/solution.py
@@ -267,7 +267,7 @@
                 pad_ref[k, t, z, PAD : PAD + n_y, :] = val
             return carry
 
-        lax.fori_loop(0, n_t, vert_inner, 0)
+        lax.fori_loop(0, n_t, vert_inner, 0, unroll=3)
         if first:
             barrier = pltpu.get_barrier_semaphore()
             for dev in ((lon, lat, partner), (left, lat, lev), (right, lat, lev)):

time: 39.8 us -> 39.7 us (level)
  no operation moved by 1% of the time
where the time goes in v18:
time: 39.7 us; the launch traced here: 39 us
  Pallas kernels  38.4 us (97%)
  between operations  0.64 us (2%)
    pallas_call x1, Pallas kernels, shards(): pl.pallas_call(kernel, out_shape=(jax.ShapeDtypeStruct(adjoint_in.shape,...  36.5 us
    pallas_call x1, Pallas kernels, shards(): pl.pallas_call(hand_over, out_shape=(jax.ShapeDtypeStruct(adj_out.shape,...  1.92 us

profile of v18, /device:TPU:5, one launch (start us, length us, event | category | flops | bytes accessed | tf_op | source)
XLA Modules:
  0.0 39.0 jit_solution(5937866731751628159)
XLA Ops:
  0.6 36.5 %shard_map.122 = (f32[9,8,16,128]{3,2,1,0:T(8,128)}, f32[3,16,128]{2,1,0:T(8,128)}) custom-call(f32[9,8,16,128]{3,2,1,0:T(8,128)} %adj_hbm.1, bf16[3,9,8,16,128]{4,3,2,1,0:T(8,128)(2,1)} %traj_hbm.1, f32[2,8,16,128]{3,2,1,0:T(8,128)} %cour_hbm.1, f32[8,16,128]{2,1,0:T(8,128)} %mix_hbm.1, s32[16,128]{1,0:T(8,128)} %land_hbm.1, s32[16,128]{1,0:T(8,128)} %srcm_hbm.1, ...), custom_call_target="tpu_custom_call" | custom-call | tf_op jit(solution)/shard_map/pallas_call | solution.py:475
  37.1 1.9 %shard_map.123 = (f32[9,8,16,128]{3,2,1,0:T(8,128)}, f32[3,16,128]{2,1,0:T(8,128)}) custom-call(f32[9,8,16,128]{3,2,1,0:T(8,128)} %get-tuple-element.4.adj_hbm, f32[3,16,128]{2,1,0:T(8,128)} %get-tuple-element.5.emis_hbm), custom_call_target="tpu_custom_call" | custom-call | tf_op jit(solution)/shard_map/pallas_call | solution.py:522

commit v19 on v16

--- a/solution.py
+++ b/solution.py
@@ -404,7 +404,7 @@
                 out_ref[t, z] = out_ref[t, z] + corr
             return carry
 
-        lax.fori_loop(0, n_t, lon_edges, 0)
+        lax.fori_loop(0, n_t, lon_edges, 0, unroll=3)
 
         @pl.when(has_up)
         def _():

time: 39.8 us -> 37.1 us (0.932)
  Pallas kernels: 38.4 us -> 36.1 us
    pallas_call x1, Pallas kernels: 36.5 us -> 34.2 us  [shards(): pl.pallas_call(kernel, out_shape=(jax.ShapeDtypeStruct(adjoint_in.shape,...]
where the time goes in v19:
time: 37.1 us; the launch traced here: 36.8 us
  Pallas kernels  36.1 us (97%)
  between operations  0.64 us (2%)
    pallas_call x1, Pallas kernels, shards(): pl.pallas_call(kernel, out_shape=(jax.ShapeDtypeStruct(adjoint_in.shape,...  34.2 us
    pallas_call x1, Pallas kernels, shards(): pl.pallas_call(hand_over, out_shape=(jax.ShapeDtypeStruct(adj_out.shape,...  1.92 us

profile of v19, /device:TPU:5, one launch (start us, length us, event | category | flops | bytes accessed | tf_op | source)
XLA Modules:
  0.0 36.8 jit_solution(13197343441189575373)
XLA Ops:
  0.6 34.2 %shard_map.122 = (f32[9,8,16,128]{3,2,1,0:T(8,128)}, f32[3,16,128]{2,1,0:T(8,128)}) custom-call(f32[9,8,16,128]{3,2,1,0:T(8,128)} %adj_hbm.1, bf16[3,9,8,16,128]{4,3,2,1,0:T(8,128)(2,1)} %traj_hbm.1, f32[2,8,16,128]{3,2,1,0:T(8,128)} %cour_hbm.1, f32[8,16,128]{2,1,0:T(8,128)} %mix_hbm.1, s32[16,128]{1,0:T(8,128)} %land_hbm.1, s32[16,128]{1,0:T(8,128)} %srcm_hbm.1, ...), custom_call_target="tpu_custom_call" | custom-call | tf_op jit(solution)/shard_map/pallas_call | solution.py:475
  34.9 1.9 %shard_map.123 = (f32[9,8,16,128]{3,2,1,0:T(8,128)}, f32[3,16,128]{2,1,0:T(8,128)}) custom-call(f32[9,8,16,128]{3,2,1,0:T(8,128)} %get-tuple-element.4.adj_hbm, f32[3,16,128]{2,1,0:T(8,128)} %get-tuple-element.5.emis_hbm), custom_call_target="tpu_custom_call" | custom-call | tf_op jit(solution)/shard_map/pallas_call | solution.py:522

commit v20 on v19

--- a/solution.py
+++ b/solution.py
@@ -379,7 +379,7 @@
                 out_ref[t, z] = a + lon_part + lat_part
             return carry
 
-        lax.fori_loop(0, n_t, transport, 0)
+        lax.fori_loop(0, n_t, transport, 0, unroll=3)
 
         lon_right.wait()
         lon_left.wait()

time: 37.1 us -> 37.1 us (level)
  no operation moved by 1% of the time
where the time goes in v20:
time: 37.1 us; the launch traced here: 36.8 us
  Pallas kernels  36.1 us (97%)
  between operations  0.64 us (2%)
    pallas_call x1, Pallas kernels, shards(): pl.pallas_call(kernel, out_shape=(jax.ShapeDtypeStruct(adjoint_in.shape,...  34.2 us
    pallas_call x1, Pallas kernels, shards(): pl.pallas_call(hand_over, out_shape=(jax.ShapeDtypeStruct(adj_out.shape,...  1.92 us

profile of v20, /device:TPU:5, one launch (start us, length us, event | category | flops | bytes accessed | tf_op | source)
XLA Modules:
  0.0 36.8 jit_solution(527520437503158443)
XLA Ops:
  0.6 34.2 %shard_map.122 = (f32[9,8,16,128]{3,2,1,0:T(8,128)}, f32[3,16,128]{2,1,0:T(8,128)}) custom-call(f32[9,8,16,128]{3,2,1,0:T(8,128)} %adj_hbm.1, bf16[3,9,8,16,128]{4,3,2,1,0:T(8,128)(2,1)} %traj_hbm.1, f32[2,8,16,128]{3,2,1,0:T(8,128)} %cour_hbm.1, f32[8,16,128]{2,1,0:T(8,128)} %mix_hbm.1, s32[16,128]{1,0:T(8,128)} %land_hbm.1, s32[16,128]{1,0:T(8,128)} %srcm_hbm.1, ...), custom_call_target="tpu_custom_call" | custom-call | tf_op jit(solution)/shard_map/pallas_call | solution.py:475
  34.9 1.9 %shard_map.123 = (f32[9,8,16,128]{3,2,1,0:T(8,128)}, f32[3,16,128]{2,1,0:T(8,128)}) custom-call(f32[9,8,16,128]{3,2,1,0:T(8,128)} %get-tuple-element.4.adj_hbm, f32[3,16,128]{2,1,0:T(8,128)} %get-tuple-element.5.emis_hbm), custom_call_target="tpu_custom_call" | custom-call | tf_op jit(solution)/shard_map/pallas_call | solution.py:522
